TPU v7x, 128 devices: a whole 4x4x4 slice. The times are simulated.
128 devices in a mesh: seq: 4 (over x_hi, core), blk: 32 (over x_lo, z, y).
Axes of the slice: x: 4 (x_hi: 2, x_lo: 2; x = x_hi * 2 + x_lo), y: 4, z: 4, core: 2. Of those that a mesh axis runs over, the one named last changes fastest.
Arguments:
- residual_in: bfloat16 [32, 512, 2048], P('blk', 'seq'), may hold values from -6 to 6
- segment_ids: int32 [32, 512], P('blk'), may hold values from 0 to 2, never falling along the last dimension, each value on 1 to 256 neighbouring positions
- attn_gain: bfloat16 [2048], replicated, may hold values from 0.5 to 1.5
- w_qkv: bfloat16 [2048, 16, 384], P(None, 'seq')
- w_out: bfloat16 [16, 128, 2048], P('seq'), may hold values from -0.125 to 0.125
- ffn_gain: bfloat16 [2048], replicated, may hold values from 0.5 to 1.5
- w_router: bfloat16 [2048, 32], replicated, may hold values from -0.125 to 0.125
- routes: int32 [32, 512, 8], P('blk', 'seq'), may hold values from 0 to 31, all different within a row; in each aligned block of 128 rows (0 to 127, 128 to 255, ..., all dimensions but the last counted through in order) at most 48 rows name the same one
- w_gate_up: bfloat16 [32, 2048, 2048], P('blk'), may hold values from -0.125 to 0.125
- w_down: bfloat16 [32, 1024, 2048], P('blk'), may hold values from -0.1875 to 0.1875
- page_owner: int32 [32, 32], P('blk'), may hold values from 0 to 31, each once within a row
Outputs:
- residual_out: bfloat16 [32, 512, 2048], P('blk', 'seq')
- kv_cache: bfloat16 [32, 32, 16, 4096], P('blk', None, None, 'seq')
Inputs may be any that keep to these rules, and one draw needn't show every extreme that they name: `segment_ids`: within a pack the numbers never fall; 1 to 3 prompts a pack, the longest exactly 256 tokens. `routes`: each token names 8 different experts; among the 128 tokens of one device no expert is named more than 48 times, a bound that some block reaches. `page_owner`: each row is a permutation.
All inputs are finite; a program needn't handle non-finite values.
Results may differ from a plain program's by a relative error of at most 0.025.
Values may be sent and summed in bfloat16 or wider, within the bound.
A program may use at most 128 MiB of HBM per device.

v0:
```python
import math

import jax
import jax.numpy as jnp
from jax import lax
from jax.sharding import PartitionSpec as P

EPS = 1e-06


def rms_norm(value, gain):
    wide = value.astype(jnp.float32)
    scale = lax.rsqrt(jnp.mean(wide * wide, axis=-1, keepdims=True) + EPS)
    return (wide * scale * gain.astype(jnp.float32)).astype(jnp.bfloat16)


def on_device(
    residual_in,
    segment_ids,
    attn_gain,
    w_qkv,
    w_out,
    ffn_gain,
    w_router,
    routes,
    w_gate_up,
    w_down,
    page_owner,
):
    local_rows = residual_in[0]
    tok_dev = local_rows.shape[0]
    heads_here = w_qkv.shape[1]
    head_dim = w_out.shape[1]
    blk_count = lax.axis_size("blk")
    normed = rms_norm(local_rows, attn_gain)
    w_flat = w_qkv.reshape(w_qkv.shape[0], heads_here * 3 * head_dim)
    qkv = jnp.dot(
        lax.all_gather(normed, "seq", axis=0, tiled=True),
        w_flat,
        preferred_element_type=jnp.float32,
    ).astype(jnp.bfloat16)
    group_len = qkv.shape[0]
    qkv = qkv.reshape(group_len, heads_here, 3 * head_dim)
    query = qkv[:, :, :head_dim]
    key_rows = qkv[:, :, head_dim : 2 * head_dim]
    value_rows = qkv[:, :, 2 * head_dim :]
    scores = jnp.einsum(
        "qhd,khd->hqk", query, key_rows, preferred_element_type=jnp.float32
    ) / math.sqrt(head_dim)
    segment_row = segment_ids[0]
    same = segment_row[:, None] == segment_row[None, :]
    scores = jnp.where(same[None], scores, jnp.float32(-1e30))
    top = jnp.max(scores, axis=-1, keepdims=True)
    weights = jnp.exp(scores - top)
    probs = (weights / jnp.sum(weights, axis=-1, keepdims=True)).astype(jnp.bfloat16)
    context = jnp.einsum(
        "hqk,khd->qhd", probs, value_rows, preferred_element_type=jnp.float32
    ).astype(jnp.bfloat16)
    context_flat = context.reshape(group_len, heads_here * head_dim)
    w_out_flat = w_out.reshape(heads_here * head_dim, w_out.shape[2])
    mixed = lax.psum_scatter(
        jnp.dot(context_flat, w_out_flat, preferred_element_type=jnp.float32).astype(jnp.bfloat16),
        "seq",
        scatter_dimension=0,
        tiled=True,
    ).astype(jnp.float32)
    resid = (local_rows.astype(jnp.float32) + mixed).astype(jnp.bfloat16)
    kv_rows = qkv[:, :, head_dim:].reshape(group_len, heads_here * 2 * head_dim)
    page_len = group_len // blk_count
    pages = kv_rows.reshape(blk_count, page_len, kv_rows.shape[1])
    owners = page_owner[0]
    places = jnp.arange(blk_count, dtype=jnp.int32)
    match = owners[None, :] == places[:, None]
    source_page = jnp.sum(jnp.where(match, places[None, :], 0), axis=1)
    outgoing = jnp.take(pages, source_page, axis=0)
    arrived = lax.all_to_all(outgoing, "blk", split_axis=0, concat_axis=0, tiled=True)
    kv_cache = arrived[None]
    ffn_in = rms_norm(resid, ffn_gain)
    logits = jnp.dot(ffn_in, w_router, preferred_element_type=jnp.float32)
    gates = jax.nn.sigmoid(logits).astype(jnp.bfloat16)
    expert_count = w_router.shape[1]
    route_rows = routes[0]
    expert_ids = jnp.arange(expert_count, dtype=jnp.int32)
    chosen = jnp.any(route_rows[:, :, None] == expert_ids[None, None, :], axis=1)
    dense_gate = jnp.where(chosen, gates, jnp.zeros_like(gates))
    capacity = tok_dev * 3 // 8
    slots = jnp.arange(capacity, dtype=jnp.int32)
    row_ids = jnp.arange(tok_dev, dtype=jnp.int32)
    gate_up = w_gate_up[0]
    down = w_down[0]
    ff_width = down.shape[0]
    all_rows, all_gates = (
        lax.all_gather(ffn_in, "blk", axis=0, tiled=True),
        lax.all_gather(dense_gate, "blk", axis=0, tiled=True),
    )
    own_expert = lax.axis_index("blk") * w_gate_up.shape[0]
    gate_col = lax.dynamic_slice_in_dim(all_gates, own_expert, 1, 1)[:, 0]
    blocks = tok_dev * lax.axis_size("blk") // tok_dev
    active = (gate_col > 0).reshape(blocks, tok_dev)
    rank = jnp.cumsum(active.astype(jnp.int32), axis=1) - 1
    hit = active[:, None, :] & (rank[:, None, :] == slots[None, :, None])
    slot_row = jnp.sum(jnp.where(hit, row_ids[None, None, :], 0), axis=2)
    block_ids = jnp.arange(blocks, dtype=jnp.int32)
    picked_index = (block_ids[:, None] * tok_dev + slot_row).reshape(-1)
    expert_rows = jnp.take(all_rows, picked_index, axis=0)
    both = jnp.dot(expert_rows, gate_up, preferred_element_type=jnp.float32)
    hidden = (jax.nn.silu(both[:, :ff_width]) * both[:, ff_width:]).astype(jnp.bfloat16)
    output = jnp.dot(hidden, down, preferred_element_type=jnp.float32)
    weighted = (jnp.take(gate_col, picked_index).astype(jnp.float32)[:, None] * output).astype(
        jnp.bfloat16
    )
    back_index = (block_ids[:, None] * capacity + jnp.clip(rank, 0, capacity - 1)).reshape(-1)
    per_row = jnp.take(weighted, back_index, axis=0)
    combined = lax.psum_scatter(
        jnp.where(
            active.reshape(-1)[:, None], per_row.astype(jnp.float32), jnp.float32(0.0)
        ).astype(jnp.bfloat16),
        "blk",
        scatter_dimension=0,
        tiled=True,
    ).astype(jnp.float32)
    residual_out = (resid.astype(jnp.float32) + combined).astype(jnp.bfloat16)[None]
    return (residual_out, kv_cache)


def solution(mesh):
    in_specs = (
        P("blk", "seq", None),
        P("blk", None),
        P(),
        P(None, "seq", None),
        P("seq", None, None),
        P(),
        P(),
        P("blk", "seq", None),
        P("blk", None, None),
        P("blk", None, None),
        P("blk", None),
    )
    out_specs = (P("blk", "seq", None), P("blk", None, None, "seq"))
    return jax.shard_map(
        on_device, mesh=mesh, in_specs=in_specs, out_specs=out_specs, check_vma=False
    )
```

profile of v0, /device:TPU:0, one launch (start us, length us, event | category | flops | bytes accessed | tf_op | source)
XLA Modules:
  0.0 624.2 jit_solution(5061057144327013314)
XLA Ops:
  7.2 0.0 all-gather.3.cloned.1.call-start
  7.2 1.4 fusion.26
  8.6 0.7 convert_element_type.77
  9.3 2.0 fusion.28
  11.3 0.0 all-gather.3.cloned.1.call-update
  11.3 0.0 reduce-scatter.3.cloned.1.call-start
  11.4 6.6 %copy.29 = bf16[256,8,4,384]{3,1,2,0:T(8,128)(2,1)} copy(bf16[256,8,4,384]{3,2,1,0:T(4,128)(2,1)} %bitcast.48) | data formatting | bytes 12582912
  18.0 0.2 broadcast_compare_fusion
  18.2 22.3 %all-gather.3.cloned.1.call-done = bf16[512,2048]{1,0:T(8,128)(2,1)} async-done(((bf16[128,2048]{1,0:T(8,128)(2,1)}), bf16[512,2048]{1,0:T(8,128)(2,1)}) %all-gather.3.cloned.1.call-update) | async-done | bytes 2097168 | tf_op jit(solution)/shard_map/all_gather | solution.py:38
  40.6 8.1 %convolution_convert_fusion = bf16[512,1536]{1,0:T(8,128)(2,1)} fusion(bf16[512,2048]{1,0:T(8,128)(2,1)} %all-gather.3.cloned.1.call-done, bf16[2048,1536]{1,0:T(8,128)(2,1)} %bitcast.49), kind=kOutput, calls=%fused_computation.21 | convolution fusion | flops 3222011904 | bytes 9961472 | tf_op jit(solution)/shard_map/dot_general | solution.py:37
  48.6 3.9 reshape.213
  52.6 1.9 fusion.44
  54.5 0.7 fusion.32
  55.2 3.9 fusion.45
  59.2 5.3 bitcast_convert_fusion
  64.4 0.0 reduce-scatter.3.cloned.1.call-update
  64.4 0.0 all-gather.5.cloned.1.call-start
  64.5 37.9 %reduce-scatter.3.cloned.1.call-done = bf16[128,2048]{1,0:T(8,128)(2,1)} async-done(((bf16[512,2048]{1,0:T(8,128)(2,1)}), bf16[128,2048]{1,0:T(8,128)(2,1)}) %reduce-scatter.3.cloned.1.call-update) | async-done | bytes 524304 | tf_op jit(solution)/shard_map/reduce_scatter | solution.py:61
  102.4 1.3 fusion.22
  103.7 2.0 fusion.24
  105.7 0.0 reduce-scatter.5.cloned.1.call-start
  105.9 1.3 fusion.21
  107.2 83.1 %all_gather.10 = bf16[4096,32]{0,1:T(8,128)(2,1)S(1)} all-gather(bf16[128,32]{0,1:T(8,128)(2,1)S(1)} %fusion.21), channel_id=1, replica_groups=mesh['seq'=4,'blk'=32] {'blk'}, dimensions={0}, use_global_device_ids=true | all-gather | bytes 270336 | tf_op jit(solution)/shard_map/all_gather | solution.py:94
  190.3 0.1 compare_reduce_fusion
  190.4 0.3 reduce_window_sum.11
  190.7 0.6 select_reduce_fusion
  191.3 0.1 broadcast_add_fusion
  191.4 0.1 add.189
  191.5 0.1 add.186
  191.5 0.1 dynamic-slice_reduce_fusion
  191.6 9.6 %gather_fusion = bf16[1536]{0:T(1024)(128)(2,1)S(1)} fusion(bf16[4096]{0:T(1024)(128)(2,1)S(1)} %dynamic-slice_reduce_fusion, s32[2048]{0:T(1024)S(1)} %pad_clamp_fusion), kind=kCustom, calls=%fused_computation | custom fusion | bytes 12288 | tf_op jit(solution)/shard_map/jit(_take)/gather | solution.py:109
  201.3 0.1 compare_and_fusion
  201.4 97.4 %all-gather.5.cloned.1.call-done = bf16[4096,2048]{1,0:T(8,128)(2,1)} async-done(((bf16[128,2048]{1,0:T(8,128)(2,1)}), bf16[4096,2048]{1,0:T(8,128)(2,1)}) %all-gather.5.cloned.1.call-update) | async-done | bytes 16777232 | tf_op jit(solution)/shard_map/all_gather | solution.py:93
  298.8 20.7 %gather_fusion.1 = bf16[1536,2048]{1,0:T(8,128)(2,1)} fusion(bf16[4096,2048]{1,0:T(8,128)(2,1)} %all-gather.5.cloned.1.call-done, s32[2048]{0:T(1024)S(1)} %pad_clamp_fusion), kind=kCustom, calls=%fused_computation.1 | custom fusion | bytes 12589056 | tf_op jit(solution)/shard_map/jit(_take)/gather | solution.py:105
  319.4 18.4 %fusion.1 = f32[1536,2048]{1,0:T(8,128)S(1)} fusion(bf16[1,2048,2048]{2,1,0:T(8,128)(2,1)} %param.19, bf16[1536,2048]{1,0:T(8,128)(2,1)} %gather_fusion.1, pred[1536]{0:T(1024)(128)(4,1)S(1)} %get-tuple-element.5), kind=kOutput, calls=%fused_computation.7 | convolution fusion | flops 12888047616 | bytes 27264512 | tf_op jit(solution)/shard_map/dot_general | solution.py:106
  337.8 8.8 %multiply_convert_fusion = bf16[1536,2048]{1,0:T(8,128)(2,1)} fusion(f32[1536]{0:T(1024)S(1)} %get-tuple-element.4, bf16[1,1024,2048]{2,1,0:T(8,128)(2,1)S(1)} %copy-done.8, f32[1536,2048]{1,0:T(8,128)S(1)} %fusion.1), kind=kOutput, calls=%fused_computation.6 | convolution fusion | flops 6458179584 | bytes 23074816 | tf_op jit(solution)/shard_map/dot_general | solution.py:108
  346.6 35.1 %gather_fusion.2 = bf16[4096,2048]{1,0:T(8,128)(2,1)} fusion(bf16[1536,2048]{1,0:T(8,128)(2,1)} %multiply_convert_fusion, s32[4096]{0:T(1024)S(1)} %broadcast_clamp_fusion), kind=kCustom, calls=%fused_computation.2 | custom fusion | bytes 33570816 | tf_op jit(solution)/shard_map/jit(_take)/gather | solution.py:113
  381.7 16.1 %select_convert_fusion = bf16[4096,2048]{1,0:T(8,128)(2,1)} fusion(bf16[4096,2048]{1,0:T(8,128)(2,1)} %gather_fusion.2, pred[4096]{0:T(1024)(128)(4,1)S(1)} %get-tuple-element.2, pred[4096]{0:T(1024)(128)(4,1)S(1)} %compare_reduce_fusion), kind=kLoop, calls=%fused_computation.5 | loop fusion | flops 33554432 | bytes 33562624 | tf_op jit(solution)/shard_map/convert_element_type | solution.py:117
  397.8 0.6 copy-done.9
  398.5 0.1 select_reduce_fusion.1
  398.6 2.7 slice.37
  401.3 2.6 reshape_reshape.3
  403.9 2.8 gather_fusion.3
  406.7 1.4 broadcast_select_fusion
  408.1 185.8 %all_to_all.5 = bf16[32,16,1024]{2,1,0:T(8,128)(2,1)} all-to-all(bf16[32,16,1024]{2,1,0:T(8,128)(2,1)S(1)} %broadcast_select_fusion), channel_id=1, replica_groups=mesh['seq'=4,'blk'=32] {'blk'}, dimensions={0} | all-to-all | bytes 2097152 | tf_op jit(solution)/shard_map/all_to_all | solution.py:76
  593.9 19.3 %reduce-scatter.5.cloned.1.call-done = bf16[128,2048]{1,0:T(8,128)(2,1)} async-done(((bf16[4096,2048]{1,0:T(8,128)(2,1)}), bf16[128,2048]{1,0:T(8,128)(2,1)}) %reduce-scatter.5.cloned.1.call-update) | async-done | bytes 524304 | tf_op jit(solution)/shard_map/reduce_scatter | solution.py:114
  613.2 2.1 fusion.31
  615.3 2.3 copy.38
  (37 shorter events, 0.2 us)
Async XLA Ops:
  7.2 52.0 %copy-start = (bf16[4,128,2048]{2,1,0:T(8,128)(2,1)S(1)}, bf16[4,128,2048]{2,1,0:T(8,128)(2,1)}, u32[]{:S(2)}) copy-start(bf16[4,128,2048]{2,1,0:T(8,128)(2,1)} %param.15) | copy-start | bytes 6291460
  7.2 33.4 %all-gather.3.cloned.1.call-start = ((), (), s32[]{:S(2)}) async-start(), calls=%async_computation.3 | async-start | bytes 2621440 | tf_op jit(solution)/shard_map/all_gather | solution.py:38
  11.3 91.0 %reduce-scatter.3.cloned.1.call-start = ((), (), s32[]{:S(2)}) async-start(), calls=%async_computation.4 | async-start | bytes 2621440 | tf_op jit(solution)/shard_map/reduce_scatter | solution.py:61
  11.4 6.6 %copy-start.5 = (s32[1,512]{1,0:T(1,128)S(1)}, s32[1,512]{1,0:T(1,128)}, u32[]{:S(2)}) copy-start(s32[1,512]{1,0:T(1,128)} %param.12) | copy-start | bytes 6148
  59.1 5.4 copy-start.6
  59.1 43.2 %copy-start.2 = (bf16[1,128,2048]{2,1,0:T(8,128)(2,1)S(1)}, bf16[1,128,2048]{2,1,0:T(8,128)(2,1)}, u32[]{:S(2)}) copy-start(bf16[1,128,2048]{2,1,0:T(8,128)(2,1)} %param.11) | copy-start | bytes 1572868
  59.1 46.7 %copy-start.7 = (s32[1,128,8]{1,2,0:T(8,128)S(1)}, s32[1,128,8]{1,2,0:T(8,128)}, u32[]{:S(2)}) copy-start(s32[1,128,8]{1,2,0:T(8,128)} %param.18) | copy-start | bytes 12292
  59.1 46.7 %copy-start.4 = (bf16[2048,32]{0,1:T(8,128)(2,1)S(1)}, bf16[2048,32]{0,1:T(8,128)(2,1)}, u32[]{:S(2)}) copy-start(bf16[2048,32]{0,1:T(8,128)(2,1)} %param.17) | copy-start | bytes 393220
  64.4 234.3 %all-gather.5.cloned.1.call-start = ((), (), s32[]{:S(2)}) async-start(), calls=%async_computation.5 | async-start | bytes 17301504 | tf_op jit(solution)/shard_map/all_gather | solution.py:93
  105.7 507.5 %reduce-scatter.5.cloned.1.call-start = ((), (), s32[]{:S(2)}) async-start(), calls=%async_computation.6 | async-start | bytes 17301504 | tf_op jit(solution)/shard_map/reduce_scatter | solution.py:114
  319.4 18.4 %copy-start.8 = (bf16[1,1024,2048]{2,1,0:T(8,128)(2,1)S(1)}, bf16[1,1024,2048]{2,1,0:T(8,128)(2,1)}, u32[]{:S(2)}) copy-start(bf16[1,1024,2048]{2,1,0:T(8,128)(2,1)} %param.20) | copy-start | bytes 12582916
  397.8 0.7 copy-start.9
  397.8 215.4 %copy-start.3 = (bf16[128,2048]{1,0:T(8,128)(2,1)S(1)}, bf16[128,2048]{1,0:T(8,128)(2,1)}, u32[]{:S(2)}) copy-start(bf16[128,2048]{1,0:T(8,128)(2,1)} %reduce-scatter.3.cloned.1.call-done) | copy-start | bytes 1572868
  398.6 219.0 %copy-start.1 = (bf16[4,128,2048]{2,1,0:T(8,128)(2,1)S(1)}, bf16[4,128,2048]{2,1,0:T(8,128)(2,1)}, u32[]{:S(2)}) copy-start(bf16[4,128,2048]{2,1,0:T(8,128)(2,1)} %param.15) | copy-start | bytes 6291460
Sparse Core Ops, SparseCore 0:
  11.5 29.0 all-gather.2
  64.6 37.7 reduce-scatter.2
  105.9 192.8 all-gather.4
  397.9 215.2 reduce-scatter.4
where the time goes:
time: 625 us; the launch traced here: 624 us
  blocking collectives  269 us (43%)
  waiting for transfers between devices  177 us (28%)
  local copies, waits for them, and re-layouts  89.2 us (14%)
  matrix products  42.5 us (7%)
  other arithmetic  32.5 us (5%)
  between operations  14 us (2%)
    all_to_all x1, blocking collectives, on_device(): lax.all_to_all(outgoing, 'blk', split_axis=0, concat_axis=0, tiled=True)  186 us
    all_gather x1, waiting for transfers between devices, on_device(): lax.all_gather(ffn_in, 'blk', axis=0, tiled=True)  97.4 us
    all_gather x1, blocking collectives, on_device(): lax.all_gather(dense_gate, 'blk', axis=0, tiled=True)  83.1 us
    reduce_scatter x1, waiting for transfers between devices, on_device(): lax.psum_scatter(jnp.dot(context_flat, w_out_flat, preferred_element_type...  37.9 us
    gather x1, local copies, waits for them, and re-layouts, on_device(): per_row = jnp.take(weighted, back_index, axis=0)  35.1 us
    all_gather x1, waiting for transfers between devices, on_device(): lax.all_gather(normed, 'seq', axis=0, tiled=True)  22.3 us
    gather x1, local copies, waits for them, and re-layouts, on_device(): expert_rows = jnp.take(all_rows, picked_index, axis=0)  20.7 us
    reduce_scatter x1, waiting for transfers between devices, on_device(): lax.psum_scatter(jnp.where(active.reshape(-1)[:, None], per_row.astype(jn...  19.3 us
  transfers between devices with their start and end apart: 4, of which 4 were waited for; matrix products, arithmetic and copies ran while one was open for 5% of the time, Pallas kernels for 0%

commit v1 on v0

v1 whole, which is shorter than its diff:
```python
import math

import jax
import jax.numpy as jnp
from jax import lax
from jax.experimental import pallas as pl
from jax.experimental.pallas import tpu as pltpu
from jax.sharding import PartitionSpec as P

EPS = 1e-06


def rms_norm(value, gain):
    wide = value.astype(jnp.float32)
    scale = lax.rsqrt(jnp.mean(wide * wide, axis=-1, keepdims=True) + EPS)
    return (wide * scale * gain.astype(jnp.float32)).astype(jnp.bfloat16)


NPOS = 32
CAP = 48
GRP = 8
NGRP = NPOS // GRP
ROWS = GRP * CAP
TILE = 256
MESH = pl.DeviceIdType.MESH


def step_of(position):
    k = lax.rem(position * 3, NPOS)
    dx, dz, dy = lax.div(k, 16), lax.rem(lax.div(k, 4), 4), lax.rem(k, 4)
    return dx, dz, dy


def peer(blk, seq, position, sign, swap=True):
    dx, dz, dy = step_of(position)
    x, z, y = lax.div(blk, 16), lax.rem(lax.div(blk, 4), 4), lax.rem(blk, 4)
    x = lax.rem(x + dx, 2)
    z = lax.rem(z + 4 + sign * dz, 4)
    y = lax.rem(y + 4 + sign * dy, 4)
    other = 2 * dx * (1 - lax.rem(dy + dz, 2)) if swap else 0
    return lax.rem(seq + other, 4), (x * 4 + z) * 4 + y


def experts_kernel(
    resid_ref,
    gain_ref,
    router_ref,
    routes_ref,
    pages_ref,
    gate_up_hbm,
    down_hbm,
    out_ref,
    kv_ref,
    normed,
    rank,
    gates,
    packed,
    recv,
    sent,
    ret,
    hidden,
    gate_up,
    down,
    total,
    weight_sems,
    kv_local_sem,
    out_send,
    out_recv,
    back_send,
    back_recv,
    kv_send,
    kv_recv,
):
    blk = lax.axis_index("blk")
    seq = lax.axis_index("seq")
    load_gate_up = pltpu.make_async_copy(gate_up_hbm, gate_up, weight_sems.at[0])
    load_down = pltpu.make_async_copy(down_hbm, down, weight_sems.at[1])
    load_gate_up.start()
    load_down.start()

    barrier = pltpu.get_barrier_semaphore()

    def greet(j, _):
        pl.semaphore_signal(
            barrier, inc=1, device_id=peer(blk, seq, j, 1), device_id_type=MESH
        )
        return 0

    lax.fori_loop(1, NPOS, greet, 0)

    def greet_swapped(i, _):
        z, y = lax.div(i, 2), lax.rem(i, 2) * 2 + lax.rem(lax.div(i, 2), 2)
        far = (lax.rem(lax.div(blk, 16) + 1, 2)) * 16
        far = far + lax.rem(lax.rem(lax.div(blk, 4), 4) + z, 4) * 4
        far = far + lax.rem(lax.rem(blk, 4) + y, 4)
        pl.semaphore_signal(
            barrier, inc=1, device_id=(seq, far), device_id_type=MESH
        )
        return 0

    lax.fori_loop(0, 8, greet_swapped, 0)

    wide = resid_ref[...].astype(jnp.float32)
    scale = lax.rsqrt(jnp.mean(wide * wide, axis=-1, keepdims=True) + EPS)
    normed[...] = (wide * scale * gain_ref[...].astype(jnp.float32)).astype(jnp.bfloat16)

    tokens = routes_ref.shape[1]
    place = lax.broadcasted_iota(jnp.int32, (NPOS, 1), 0)
    dx, dz, dy = step_of(place)
    expert = lax.rem(lax.div(blk, 16) + dx, 2) * 16
    expert = expert + lax.rem(lax.rem(lax.div(blk, 4), 4) + dz, 4) * 4
    expert = expert + lax.rem(lax.rem(blk, 4) + dy, 4)
    chosen = jnp.zeros((NPOS, tokens), jnp.int32)
    for k in range(routes_ref.shape[0]):
        chosen = jnp.where(routes_ref[k : k + 1, :] == expert, 1, chosen)
    upto = lax.broadcasted_iota(jnp.int32, (tokens, tokens), 0) <= lax.broadcasted_iota(
        jnp.int32, (tokens, tokens), 1
    )
    count = jnp.dot(
        chosen.astype(jnp.bfloat16),
        jnp.where(upto, 1.0, 0.0).astype(jnp.bfloat16),
        preferred_element_type=jnp.float32,
    ).astype(jnp.int32)
    rank[...] = jnp.where(chosen == 1, count - 1, -1)

    slot = lax.broadcasted_iota(jnp.int32, (GRP, CAP, tokens), 1)

    def hits(g):
        rows = rank[pl.ds(pl.multiple_of(g * GRP, GRP), GRP), :]
        return rows[:, None, :] == slot

    def slab(j):
        return pl.ds(pl.multiple_of(j * CAP, CAP), CAP)

    def dispatch(j):
        return pltpu.make_async_remote_copy(
            src_ref=packed.at[slab(j)],
            dst_ref=recv.at[slab(j)],
            send_sem=out_send.at[j],
            recv_sem=out_recv.at[j],
            device_id=peer(blk, seq, j, 1),
            device_id_type=MESH,
        )

    def give_back(j):
        return pltpu.make_async_remote_copy(
            src_ref=sent.at[slab(j)],
            dst_ref=ret.at[slab(j)],
            send_sem=back_send.at[j],
            recv_sem=back_recv.at[j],
            device_id=peer(blk, seq, j, -1),
            device_id_type=MESH,
        )

    def page_copy(j):
        to_seq, to_blk = peer(blk, seq, j, 1, swap=False)
        return pltpu.make_async_remote_copy(
            src_ref=pages_ref.at[to_blk],
            dst_ref=kv_ref.at[blk],
            send_sem=kv_send.at[j],
            recv_sem=kv_recv.at[j],
            device_id=(to_seq, to_blk),
            device_id_type=MESH,
        )

    def page_arrival(j):
        to_seq, from_blk = peer(blk, seq, j, -1, swap=False)
        return pltpu.make_async_remote_copy(
            src_ref=pages_ref.at[from_blk],
            dst_ref=kv_ref.at[from_blk],
            send_sem=kv_send.at[j],
            recv_sem=kv_recv.at[j],
            device_id=(to_seq, from_blk),
            device_id_type=MESH,
        )

    def pack(g):
        one_hot = jnp.where(hits(g), 1.0, 0.0).reshape(ROWS, tokens).astype(jnp.bfloat16)
        rows = pl.ds(pl.multiple_of(g * ROWS, ROWS), ROWS)

        @pl.loop(0, normed.shape[1] // 512)
        def _(n):
            cols = pl.ds(pl.multiple_of(n * 512, 512), 512)
            packed[rows, cols] = jnp.dot(
                one_hot, normed[:, cols], preferred_element_type=jnp.float32
            ).astype(jnp.bfloat16)

    pack(0)
    pl.semaphore_wait(barrier, NPOS - 1 + 8)
    recv[0:CAP, :] = packed[0:CAP, :]

    for g in range(NGRP):
        if g > 0:
            pack(g)
        lax.fori_loop(max(g * GRP, 1), (g + 1) * GRP, lambda j, _: (dispatch(j).start(), 0)[1], 0)

    own_page = pltpu.make_async_copy(pages_ref.at[blk], kv_ref.at[blk], kv_local_sem)
    own_page.start()
    lax.fori_loop(1, NPOS, lambda j, _: (page_copy(j).start(), 0)[1], 0)

    logits = jnp.dot(normed[...], router_ref[...], preferred_element_type=jnp.float32)
    by_expert = jax.nn.sigmoid(logits).astype(jnp.bfloat16)
    order = jnp.where(
        expert == lax.broadcasted_iota(jnp.int32, (NPOS, NPOS), 1), 1.0, 0.0
    ).astype(jnp.bfloat16)
    gates[...] = lax.dot_general(
        order, by_expert, (((1,), (1,)), ((), ())), preferred_element_type=jnp.float32
    )

    load_gate_up.wait()
    load_down.wait()
    ff = down.shape[0]
    width = down.shape[1]

    @pl.loop(0, NGRP)
    def _(g):
        first = jnp.where(g == 0, 1, g * GRP)
        lax.fori_loop(first, (g + 1) * GRP, lambda j, _: (dispatch(j).wait_recv(), 0)[1], 0)
        rows = pl.ds(pl.multiple_of(g * ROWS, ROWS), ROWS)

        @pl.loop(0, ff // TILE)
        def _(f):
            cols = pl.ds(pl.multiple_of(f * TILE, TILE), TILE)
            up_cols = pl.ds(pl.multiple_of(ff + f * TILE, TILE), TILE)
            gate = jnp.dot(recv[rows, :], gate_up[:, cols], preferred_element_type=jnp.float32)
            up = jnp.dot(recv[rows, :], gate_up[:, up_cols], preferred_element_type=jnp.float32)
            hidden[:, cols] = (jax.nn.silu(gate) * up).astype(jnp.bfloat16)

        @pl.loop(0, width // TILE)
        def _(n):
            cols = pl.ds(pl.multiple_of(n * TILE, TILE), TILE)
            sent[rows, cols] = jnp.dot(
                hidden[...], down[:, cols], preferred_element_type=jnp.float32
            ).astype(jnp.bfloat16)

        lax.fori_loop(first, (g + 1) * GRP, lambda j, _: (give_back(j).start(), 0)[1], 0)

    ret[0:CAP, :] = sent[0:CAP, :]
    total[...] = resid_ref[...].astype(jnp.float32)

    @pl.loop(0, NGRP)
    def _(g):
        first = jnp.where(g == 0, 1, g * GRP)
        weight = gates[pl.ds(pl.multiple_of(g * GRP, GRP), GRP), :]
        spread = jnp.where(hits(g), weight[:, None, :], 0.0).reshape(ROWS, tokens)
        spread = spread.T.astype(jnp.bfloat16)
        lax.fori_loop(first, (g + 1) * GRP, lambda j, _: (give_back(j).wait_recv(), 0)[1], 0)
        rows = pl.ds(pl.multiple_of(g * ROWS, ROWS), ROWS)

        @pl.loop(0, width // 512)
        def _(n):
            cols = pl.ds(pl.multiple_of(n * 512, 512), 512)
            total[:, cols] += jnp.dot(spread, ret[rows, cols], preferred_element_type=jnp.float32)

    out_ref[...] = total[...].astype(jnp.bfloat16)

    def drain(j, _):
        page_arrival(j).wait_recv()
        page_copy(j).wait_send()
        dispatch(j).wait_send()
        give_back(j).wait_send()
        return 0

    lax.fori_loop(1, NPOS, drain, 0)
    own_page.wait()


def experts(resid, ffn_gain, w_router, routes, pages, gate_up, down):
    tokens, width = resid.shape
    slots = NPOS * CAP
    vmem = pl.BlockSpec(memory_space=pltpu.VMEM)
    hbm = pl.BlockSpec(memory_space=pl.ANY)
    dma = pltpu.SemaphoreType.DMA
    return pl.pallas_call(
        experts_kernel,
        out_shape=(
            jax.ShapeDtypeStruct((tokens, width), jnp.bfloat16),
            jax.ShapeDtypeStruct(pages.shape, jnp.bfloat16),
        ),
        in_specs=[vmem] * 5 + [hbm] * 2,
        out_specs=(vmem, vmem),
        scratch_shapes=[
            pltpu.VMEM((tokens, width), jnp.bfloat16),
            pltpu.VMEM((NPOS, tokens), jnp.int32),
            pltpu.VMEM((NPOS, tokens), jnp.float32),
            pltpu.VMEM((slots, width), jnp.bfloat16),
            pltpu.VMEM((slots, width), jnp.bfloat16),
            pltpu.VMEM((slots, width), jnp.bfloat16),
            pltpu.VMEM((slots, width), jnp.bfloat16),
            pltpu.VMEM((ROWS, down.shape[0]), jnp.bfloat16),
            pltpu.VMEM(gate_up.shape, jnp.bfloat16),
            pltpu.VMEM(down.shape, jnp.bfloat16),
            pltpu.VMEM((tokens, width), jnp.float32),
            dma((2,)),
            dma,
            dma((NPOS,)),
            dma((NPOS,)),
            dma((NPOS,)),
            dma((NPOS,)),
            dma((NPOS,)),
            dma((NPOS,)),
        ],
        compiler_params=pltpu.CompilerParams(
            collective_id=0, has_side_effects=True, vmem_limit_bytes=58 << 20
        ),
        cost_estimate=pl.CostEstimate(
            flops=2 * slots * 3 * down.shape[0] * width,
            bytes_accessed=16 << 20,
            transcendentals=slots * down.shape[0],
        ),
    )(resid, ffn_gain.reshape(1, width), w_router, routes.T, pages, gate_up, down)


def on_device(
    residual_in,
    segment_ids,
    attn_gain,
    w_qkv,
    w_out,
    ffn_gain,
    w_router,
    routes,
    w_gate_up,
    w_down,
    page_owner,
):
    local_rows = residual_in[0]
    tok_dev = local_rows.shape[0]
    heads_here = w_qkv.shape[1]
    head_dim = w_out.shape[1]
    blk_count = lax.axis_size("blk")
    normed = rms_norm(local_rows, attn_gain)
    w_flat = w_qkv.reshape(w_qkv.shape[0], heads_here * 3 * head_dim)
    qkv = jnp.dot(
        lax.all_gather(normed, "seq", axis=0, tiled=True),
        w_flat,
        preferred_element_type=jnp.float32,
    ).astype(jnp.bfloat16)
    group_len = qkv.shape[0]
    qkv = qkv.reshape(group_len, heads_here, 3 * head_dim)
    query = qkv[:, :, :head_dim]
    key_rows = qkv[:, :, head_dim : 2 * head_dim]
    value_rows = qkv[:, :, 2 * head_dim :]
    scores = jnp.einsum(
        "qhd,khd->hqk", query, key_rows, preferred_element_type=jnp.float32
    ) / math.sqrt(head_dim)
    segment_row = segment_ids[0]
    same = segment_row[:, None] == segment_row[None, :]
    scores = jnp.where(same[None], scores, jnp.float32(-1e30))
    top = jnp.max(scores, axis=-1, keepdims=True)
    weights = jnp.exp(scores - top)
    probs = (weights / jnp.sum(weights, axis=-1, keepdims=True)).astype(jnp.bfloat16)
    context = jnp.einsum(
        "hqk,khd->qhd", probs, value_rows, preferred_element_type=jnp.float32
    ).astype(jnp.bfloat16)
    context_flat = context.reshape(group_len, heads_here * head_dim)
    w_out_flat = w_out.reshape(heads_here * head_dim, w_out.shape[2])
    mixed = lax.psum_scatter(
        jnp.dot(context_flat, w_out_flat, preferred_element_type=jnp.float32).astype(jnp.bfloat16),
        "seq",
        scatter_dimension=0,
        tiled=True,
    ).astype(jnp.float32)
    resid = (local_rows.astype(jnp.float32) + mixed).astype(jnp.bfloat16)
    kv_rows = qkv[:, :, head_dim:].reshape(group_len, heads_here * 2 * head_dim)
    page_len = group_len // blk_count
    pages = kv_rows.reshape(blk_count, page_len, kv_rows.shape[1])
    owners = page_owner[0]
    places = jnp.arange(blk_count, dtype=jnp.int32)
    match = owners[None, :] == places[:, None]
    source_page = jnp.sum(jnp.where(match, places[None, :], 0), axis=1)
    outgoing = jnp.take(pages, source_page, axis=0)
    residual_out, arrived = experts(
        resid, ffn_gain, w_router, routes[0], outgoing, w_gate_up[0], w_down[0]
    )
    return (residual_out[None], arrived[None])


def solution(mesh):
    in_specs = (
        P("blk", "seq", None),
        P("blk", None),
        P(),
        P(None, "seq", None),
        P("seq", None, None),
        P(),
        P(),
        P("blk", "seq", None),
        P("blk", None, None),
        P("blk", None, None),
        P("blk", None),
    )
    out_specs = (P("blk", "seq", None), P("blk", None, None, "seq"))
    return jax.shard_map(
        on_device, mesh=mesh, in_specs=in_specs, out_specs=out_specs, check_vma=False
    )
```

time: 625 us -> 319 us (0.51)
  the two profiles are of different devices: /device:TPU:0 before, /device:TPU:35 now
where the time goes in v1:
time: 319 us; the launch traced here: 318 us
  Pallas kernels  204 us (64%)
  waiting for transfers between devices  50.3 us (16%)
  local copies, waits for them, and re-layouts  22.7 us (7%)
  matrix products  14.2 us (4%)
  between operations  14.1 us (4%)
  other arithmetic  12.7 us (4%)
    pallas_call x1, Pallas kernels, experts(): pl.pallas_call(experts_kernel, out_shape=(jax.ShapeDtypeStruct((tokens, w...  204 us
    reduce_scatter x1, waiting for transfers between devices, on_device(): lax.psum_scatter(jnp.dot(context_flat, w_out_flat, preferred_element_type...  28.9 us
    all_gather x1, waiting for transfers between devices, on_device(): lax.all_gather(normed, 'seq', axis=0, tiled=True)  21.4 us
    unnamed x16, local copies, waits for them, and re-layouts  11.8 us
    dot_general x1, matrix products, on_device(): jnp.dot(lax.all_gather(normed, 'seq', axis=0, tiled=True), w_flat, prefer...  8.07 us
  transfers between devices with their start and end apart: 2, of which 2 were waited for; matrix products, arithmetic and copies ran while one was open for 5% of the time, Pallas kernels for 0%

profile of v1, /device:TPU:35, one launch (start us, length us, event | category | flops | bytes accessed | tf_op | source)
XLA Modules:
  0.0 318.3 jit_solution(14635842742293725424)
XLA Ops:
  7.2 0.0 copy-start
  7.2 0.0 all-gather.2.cloned.1.call-start
  7.2 0.8 convert_element_type.36
  8.1 1.2 fusion.8
  9.3 2.0 fusion.10
  11.3 0.0 all-gather.2.cloned.1.call-update
  11.3 0.0 reduce-scatter.2.cloned.1.call-start
  11.4 0.0 copy-start.3
  11.4 6.6 %copy.22 = bf16[256,8,4,384]{3,1,2,0:T(8,128)(2,1)} copy(bf16[256,8,4,384]{3,2,1,0:T(4,128)(2,1)} %bitcast.29) | data formatting | bytes 12582912
  18.0 0.0 copy-done.3
  18.0 0.2 broadcast_compare_fusion
  18.2 21.4 %all-gather.2.cloned.1.call-done = bf16[512,2048]{1,0:T(8,128)(2,1)} async-done(((bf16[128,2048]{1,0:T(8,128)(2,1)}), bf16[512,2048]{1,0:T(8,128)(2,1)}) %all-gather.2.cloned.1.call-update) | async-done | bytes 2097168 | tf_op jit(solution)/shard_map/all_gather | solution.py:335
  39.6 8.1 %convolution_convert_fusion = bf16[512,1536]{1,0:T(8,128)(2,1)} fusion(bf16[512,2048]{1,0:T(8,128)(2,1)} %all-gather.2.cloned.1.call-done, bf16[2048,1536]{1,0:T(8,128)(2,1)} %bitcast.30), kind=kOutput, calls=%fused_computation.7 | convolution fusion | flops 3222011904 | bytes 9961472 | tf_op jit(solution)/shard_map/dot_general | solution.py:334
  47.7 3.9 %reshape.77 = bf16[512,4,384]{2,1,0:T(4,128)(2,1)} reshape(bf16[512,1536]{1,0:T(8,128)(2,1)} %convolution_convert_fusion) | data formatting | bytes 3145728 | tf_op jit(solution)/shard_map/reshape | solution.py:340
  51.6 1.9 fusion.20
  53.5 0.7 fusion.12
  54.2 3.9 %fusion.21 = (f32[4,512]{1,0:T(4,128)S(1)}, f32[4,512,512]{1,2,0:T(8,128)}) fusion(f32[4,512,512]{1,2,0:T(8,128)S(1)} %fusion.12, pred[512,512]{0,1:T(8,128)(4,1)S(1)} %broadcast_compare_fusion), kind=kOutput, calls=%fused_computation.38 | output fusion | flops 6291967 | bytes 8658944 | tf_op jit(solution)/shard_map/sub | solution.py:351
  58.2 0.0 copy-done
  58.2 0.0 copy-start.2
  58.2 0.0 copy-start.4
  58.2 0.0 copy-start.5
  58.2 5.5 %bitcast_convert_fusion = bf16[512,2048]{1,0:T(8,128)(2,1)} fusion(bf16[4,128,2048]{2,1,0:T(8,128)(2,1)S(1)} %copy-done, f32[4,512,512]{1,2,0:T(8,128)} %get-tuple-element.10, f32[4,512]{1,0:T(4,128)S(1)} %get-tuple-element.9, bf16[512,4,128]{2,1,0:T(4,128)(2,1)S(1)} %get-tuple-element.6), kind=kOutput, calls=%fused_computation.2 | convolution fusion | flops 1345585152 | bytes 8921088 | tf_op jit(solution)/shard_map/dot_general | solution.py:359
  63.6 0.0 slice-start
  63.7 0.0 reduce-scatter.2.cloned.1.call-update
  63.7 0.0 copy-done.2
  63.7 1.0 copy.18.router_ref
  64.7 0.0 copy-done.4
  64.7 0.6 reshape.78.gain_ref
  65.3 0.0 copy-done.5
  65.3 0.1 select_reduce_fusion
  65.4 0.0 slice-done
  65.5 1.5 reshape_reshape.3
  67.0 0.0 copy-start.1
  67.0 2.9 gather_fusion
  69.9 2.4 broadcast_select_fusion.pages_ref
  72.2 28.9 %reduce-scatter.2.cloned.1.call-done = bf16[128,2048]{1,0:T(8,128)(2,1)} async-done(((bf16[512,2048]{1,0:T(8,128)(2,1)}), bf16[128,2048]{1,0:T(8,128)(2,1)}) %reduce-scatter.2.cloned.1.call-update) | async-done | bytes 524304 | tf_op jit(solution)/shard_map/reduce_scatter | solution.py:358
  101.2 0.0 copy-done.1
  101.2 2.0 fusion.11.resid_ref
  103.1 204.2 %shard_map.122 = (bf16[128,2048]{1,0:T(8,128)(2,1)}, bf16[32,16,1024]{2,1,0:T(8,128)(2,1)}) custom-call(bf16[128,2048]{1,0:T(8,128)(2,1)} %fusion.11.resid_ref, bf16[1,2048]{1,0:T(2,128)(2,1)} %reshape.78.gain_ref, bf16[2048,32]{1,0:T(8,128)(2,1)} %copy.18.router_ref, s32[8,128]{1,0:T(8,128)} %bitcast.36, ...), custom_call_target="tpu_custom_call" | custom-call | flops 19327352832 | bytes 16777216 | tf_op jit(solution)/shard_map/pallas_call | solution.py:274
  307.3 1.9 copy.32
  309.2 2.3 copy.33
  (4 shorter events, 0.0 us)
Async XLA Ops:
  7.2 51.0 %copy-start = (bf16[4,128,2048]{2,1,0:T(8,128)(2,1)S(1)}, bf16[4,128,2048]{2,1,0:T(8,128)(2,1)}, u32[]{:S(2)}) copy-start(bf16[4,128,2048]{2,1,0:T(8,128)(2,1)} %param.15) | copy-start | bytes 6291460
  7.2 32.4 %all-gather.2.cloned.1.call-start = ((), (), s32[]{:S(2)}) async-start(), calls=%async_computation.1 | async-start | bytes 2621440 | tf_op jit(solution)/shard_map/all_gather | solution.py:335
  11.3 89.8 %reduce-scatter.2.cloned.1.call-start = ((), (), s32[]{:S(2)}) async-start(), calls=%async_computation.2 | async-start | bytes 2621440 | tf_op jit(solution)/shard_map/reduce_scatter | solution.py:358
  11.4 6.6 %copy-start.3 = (s32[1,512]{1,0:T(1,128)S(1)}, s32[1,512]{1,0:T(1,128)}, u32[]{:S(2)}) copy-start(s32[1,512]{1,0:T(1,128)} %param.12) | copy-start | bytes 6148
  58.2 5.5 %copy-start.2 = (bf16[2048,32]{0,1:T(8,128)(2,1)S(1)}, bf16[2048,32]{0,1:T(8,128)(2,1)}, u32[]{:S(2)}) copy-start(bf16[2048,32]{0,1:T(8,128)(2,1)} %param.17) | copy-start | bytes 393220
  58.2 6.5 %copy-start.4 = (bf16[2048]{0:T(1024)(128)(2,1)S(1)}, bf16[2048]{0:T(1024)(128)(2,1)}, u32[]{:S(2)}) copy-start(bf16[2048]{0:T(1024)(128)(2,1)} %param.16) | copy-start | bytes 12292
  58.2 7.1 %copy-start.5 = (s32[1,32]{1,0:T(1,128)S(1)}, s32[1,32]{1,0:T(1,128)}, u32[]{:S(2)}) copy-start(s32[1,32]{1,0:T(1,128)} %param.21) | copy-start | bytes 388
  63.6 1.8 slice-start
  67.0 34.2 %copy-start.1 = (bf16[1,128,2048]{2,1,0:T(8,128)(2,1)S(1)}, bf16[1,128,2048]{2,1,0:T(8,128)(2,1)}, u32[]{:S(2)}) copy-start(bf16[1,128,2048]{2,1,0:T(8,128)(2,1)} %param.11) | copy-start | bytes 1572868
Sparse Core Ops, SparseCore 0:
  11.5 28.0 all-gather.1
  63.8 37.3 reduce-scatter.1

commit v2 on v1

v2 whole, which is shorter than its diff:
```python
import math

import jax
import jax.numpy as jnp
from jax import lax
from jax.experimental import pallas as pl
from jax.experimental.pallas import tpu as pltpu
from jax.sharding import PartitionSpec as P

EPS = 1e-06
NPOS = 32
CAP = 48
GRP = 8
NGRP = NPOS // GRP
ROWS = GRP * CAP
TILE = 256
HEAD = 128
PARTS = 4
SPAN = 512
MESH = pl.DeviceIdType.MESH


def step_of(position):
    k = lax.rem(position * 3, NPOS)
    dx, dz, dy = lax.div(k, 16), lax.rem(lax.div(k, 4), 4), lax.rem(k, 4)
    return dx, dz, dy


def peer(blk, seq, position, sign, swap=True):
    dx, dz, dy = step_of(position)
    x, z, y = lax.div(blk, 16), lax.rem(lax.div(blk, 4), 4), lax.rem(blk, 4)
    x = lax.rem(x + dx, 2)
    z = lax.rem(z + 4 + sign * dz, 4)
    y = lax.rem(y + 4 + sign * dy, 4)
    other = 2 * dx * (1 - lax.rem(dy + dz, 2)) if swap else 0
    return lax.rem(seq + other, 4), (x * 4 + z) * 4 + y


def layer_kernel(
    rows_ref,
    segment_ref,
    owner_ref,
    attn_gain_ref,
    ffn_gain_ref,
    router_ref,
    routes_ref,
    qkv_hbm,
    out_hbm,
    gate_up_hbm,
    down_hbm,
    out_ref,
    kv_ref,
    queries,
    keys_values,
    pages_ref,
    context,
    partial,
    near_send,
    near_recv,
    far_send,
    far_recv,
    resid,
    normed,
    rank,
    gates,
    packed,
    recv,
    sent,
    ret,
    hidden,
    gate_up,
    down,
    total,
    weight_sems,
    kv_local_sem,
    out_send,
    out_recv,
    back_send,
    back_recv,
    kv_send,
    kv_recv,
    own_sems,
    gather_send,
    gather_recv,
    pass_send,
    pass_recv,
    near_send_sems,
    near_recv_sems,
    far_send_sems,
    far_recv_sems,
):
    blk = lax.axis_index("blk")
    seq = lax.axis_index("seq")
    half = lax.div(seq, 2)
    core = lax.rem(seq, 2)
    mate = seq + 1 - 2 * core
    far = lax.rem(seq + 2, 4)
    tok = rows_ref.shape[0]
    width = rows_ref.shape[1]
    length = 4 * tok
    heads = out_hbm.shape[0] // HEAD
    w_qkv = sent.at[0:width, 0 : qkv_hbm.shape[1]]
    w_out = packed.at[0 : out_hbm.shape[0]]
    everyone = packed.at[out_hbm.shape[0] : out_hbm.shape[0] + length]
    load_qkv = pltpu.make_async_copy(qkv_hbm, w_qkv, weight_sems.at[2])
    load_out = pltpu.make_async_copy(out_hbm, w_out, weight_sems.at[3])
    load_gate_up = pltpu.make_async_copy(gate_up_hbm, gate_up, weight_sems.at[0])
    load_down = pltpu.make_async_copy(down_hbm, down, weight_sems.at[1])
    load_qkv.start()
    load_out.start()

    barrier = pltpu.get_barrier_semaphore()

    def greet(j, _):
        pl.semaphore_signal(
            barrier, inc=1, device_id=peer(blk, seq, j, 1), device_id_type=MESH
        )
        return 0

    lax.fori_loop(1, NPOS, greet, 0)

    def greet_swapped(i, _):
        z, y = lax.div(i, 2), lax.rem(i, 2) * 2 + lax.rem(lax.div(i, 2), 2)
        there = (lax.rem(lax.div(blk, 16) + 1, 2)) * 16
        there = there + lax.rem(lax.rem(lax.div(blk, 4), 4) + z, 4) * 4
        there = there + lax.rem(lax.rem(blk, 4) + y, 4)
        pl.semaphore_signal(
            barrier, inc=1, device_id=(seq, there), device_id_type=MESH
        )
        return 0

    lax.fori_loop(0, 8, greet_swapped, 0)
    for other in (mate, far):
        pl.semaphore_signal(barrier, inc=1, device_id=(other, blk), device_id_type=MESH)

    def block(index):
        return pl.ds(pl.multiple_of(index * tok, tok), tok)

    def norm(wide, gain_ref):
        scale = lax.rsqrt(jnp.mean(wide * wide, axis=-1, keepdims=True) + EPS)
        return (wide * scale * gain_ref[...].astype(jnp.float32)).astype(jnp.bfloat16)

    def send(src, dst, send_sem, recv_sem, to):
        return pltpu.make_async_remote_copy(
            src_ref=src,
            dst_ref=dst,
            send_sem=send_sem,
            recv_sem=recv_sem,
            device_id=(to, blk),
            device_id_type=MESH,
        )

    def piece(index, i):
        rows = tok // PARTS
        return everyone.at[pl.ds(pl.multiple_of(index * tok + i * rows, rows), rows)]

    everyone[block(seq), :] = norm(rows_ref[...].astype(jnp.float32), attn_gain_ref)
    pl.semaphore_wait(barrier, NPOS - 1 + 8 + 2)

    own_out = send(
        everyone.at[block(seq)], everyone.at[block(seq)], own_sems.at[0], own_sems.at[1], mate
    )
    own_in = send(
        everyone.at[block(mate)], everyone.at[block(mate)], own_sems.at[0], own_sems.at[1], mate
    )
    gather_out = [
        send(piece(seq, i), piece(seq, i), gather_send.at[i], gather_recv.at[i], far)
        for i in range(PARTS)
    ]
    gather_in = [
        send(piece(far, i), piece(far, i), gather_send.at[i], gather_recv.at[i], far)
        for i in range(PARTS)
    ]
    far_mate = lax.rem(mate + 2, 4)
    pass_out = [
        send(piece(far, i), piece(far, i), pass_send.at[i], pass_recv.at[i], mate)
        for i in range(PARTS)
    ]
    pass_in = [
        send(piece(far_mate, i), piece(far_mate, i), pass_send.at[i], pass_recv.at[i], mate)
        for i in range(PARTS)
    ]
    for copy in gather_out:
        copy.start()
    own_out.start()

    def two_blocks(index):
        return pl.ds(pl.multiple_of(index * 2 * tok, 2 * tok), 2 * tok)

    def project(index):
        rows = two_blocks(index)

        @pl.loop(0, heads // 2)
        def _(p):
            cols = pl.ds(pl.multiple_of(p * 6 * HEAD, 6 * HEAD), 6 * HEAD)
            both = jnp.dot(
                everyone[rows, :], w_qkv[:, cols], preferred_element_type=jnp.float32
            ).astype(jnp.bfloat16)
            q_cols = pl.ds(pl.multiple_of(p * 2 * HEAD, 2 * HEAD), 2 * HEAD)
            kv_cols = pl.ds(pl.multiple_of(p * 4 * HEAD, 4 * HEAD), 4 * HEAD)
            queries[rows, q_cols] = jnp.concatenate(
                [both[:, 0:HEAD], both[:, 3 * HEAD : 4 * HEAD]], axis=1
            )
            keys_values[rows, kv_cols] = jnp.concatenate(
                [both[:, HEAD : 3 * HEAD], both[:, 4 * HEAD :]], axis=1
            )

    load_qkv.wait()
    load_out.wait()
    load_gate_up.start()
    load_down.start()
    own_in.wait_recv()
    project(half)
    for i in range(PARTS):
        gather_in[i].wait_recv()
        pass_out[i].start()
    for i in range(PARTS):
        pass_in[i].wait_recv()
    project(1 - half)

    def page_copy(j):
        to_seq, to_blk = peer(blk, seq, j, 1, swap=False)
        return pltpu.make_async_remote_copy(
            src_ref=pages_ref.at[to_blk],
            dst_ref=kv_ref.at[blk],
            send_sem=kv_send.at[j],
            recv_sem=kv_recv.at[j],
            device_id=(to_seq, to_blk),
            device_id_type=MESH,
        )

    def page_arrival(j):
        to_seq, from_blk = peer(blk, seq, j, -1, swap=False)
        return pltpu.make_async_remote_copy(
            src_ref=pages_ref.at[from_blk],
            dst_ref=kv_ref.at[from_blk],
            send_sem=kv_send.at[j],
            recv_sem=kv_recv.at[j],
            device_id=(to_seq, from_blk),
            device_id_type=MESH,
        )

    page = length // NPOS
    to_row = lax.broadcasted_iota(jnp.int32, (length, length), 0)
    from_row = lax.broadcasted_iota(jnp.int32, (length, length), 1)
    moves = (lax.rem(to_row, page) == lax.rem(from_row, page)) & (
        lax.div(to_row, page) == owner_ref[...]
    )
    pages_ref[...] = (
        jnp.dot(
            jnp.where(moves, 1.0, 0.0).astype(jnp.bfloat16),
            keys_values[...],
            preferred_element_type=jnp.float32,
        )
        .astype(jnp.bfloat16)
        .reshape(pages_ref.shape)
    )
    own_page = pltpu.make_async_copy(pages_ref.at[blk], kv_ref.at[blk], kv_local_sem)
    own_page.start()
    lax.fori_loop(1, NPOS, lambda j, _: (page_copy(j).start(), 0)[1], 0)

    segment_row = segment_ref[...]
    segment_column = jnp.broadcast_to(segment_row, (HEAD, length)).T

    def attend(index):
        rows = two_blocks(index)
        picked = jnp.where(index == 0, segment_column[0 : 2 * tok], segment_column[2 * tok :])
        same = picked[:, 0:1] == segment_row

        @pl.loop(0, heads)
        def _(head):
            cols = pl.ds(pl.multiple_of(head * HEAD, HEAD), HEAD)
            k_cols = pl.ds(pl.multiple_of(head * 2 * HEAD, HEAD), HEAD)
            v_cols = pl.ds(pl.multiple_of(head * 2 * HEAD + HEAD, HEAD), HEAD)
            scores = lax.dot_general(
                queries[rows, cols],
                keys_values[:, k_cols],
                (((1,), (1,)), ((), ())),
                preferred_element_type=jnp.float32,
            ) * (1.0 / math.sqrt(HEAD))
            scores = jnp.where(same, scores, -1e30)
            weights = jnp.exp(scores - jnp.max(scores, axis=-1, keepdims=True))
            probs = (weights / jnp.sum(weights, axis=-1, keepdims=True)).astype(jnp.bfloat16)
            context[rows, cols] = jnp.dot(
                probs, keys_values[:, v_cols], preferred_element_type=jnp.float32
            ).astype(jnp.bfloat16)

    def column(n):
        return pl.ds(n * SPAN, SPAN)

    def near_copy(which, n):
        return send(
            near_send.at[which, :, column(n)],
            near_recv.at[which, :, column(n)],
            near_send_sems.at[which, n],
            near_recv_sems.at[which, n],
            mate,
        )

    def far_copy(n):
        return send(
            far_send.at[:, column(n)],
            far_recv.at[:, column(n)],
            far_send_sems.at[n],
            far_recv_sems.at[n],
            far,
        )

    def mix(which, index):
        for n in range(width // SPAN):
            partial[:, column(n)] = jnp.dot(
                context[two_blocks(index), :],
                w_out[:, column(n)],
                preferred_element_type=jnp.float32,
            )
            near_send[which, :, column(n)] = partial[block(1 - core), column(n)].astype(
                jnp.bfloat16
            )
            near_copy(which, n).start()

    def reduced(which, n):
        near_copy(which, n).wait_recv()
        return partial[block(core), column(n)] + near_recv[which, :, column(n)].astype(
            jnp.float32
        )

    attend(1 - half)
    mix(0, 1 - half)
    for n in range(width // SPAN):
        far_send[:, column(n)] = reduced(0, n).astype(jnp.bfloat16)
        far_copy(n).start()
    attend(half)
    mix(1, half)
    for n in range(width // SPAN):
        mixed = reduced(1, n)
        far_copy(n).wait_recv()
        mixed = mixed + far_recv[:, column(n)].astype(jnp.float32)
        resid[:, column(n)] = (rows_ref[:, column(n)].astype(jnp.float32) + mixed).astype(
            jnp.bfloat16
        )
    normed[...] = norm(resid[...].astype(jnp.float32), ffn_gain_ref)
    own_out.wait_send()
    for i in range(PARTS):
        gather_out[i].wait_send()
        pass_out[i].wait_send()

    tokens = tok
    place = lax.broadcasted_iota(jnp.int32, (NPOS, 1), 0)
    dx, dz, dy = step_of(place)
    expert = lax.rem(lax.div(blk, 16) + dx, 2) * 16
    expert = expert + lax.rem(lax.rem(lax.div(blk, 4), 4) + dz, 4) * 4
    expert = expert + lax.rem(lax.rem(blk, 4) + dy, 4)
    chosen = jnp.zeros((NPOS, tokens), jnp.int32)
    for k in range(routes_ref.shape[0]):
        chosen = jnp.where(routes_ref[k : k + 1, :] == expert, 1, chosen)
    upto = lax.broadcasted_iota(jnp.int32, (tokens, tokens), 0) <= lax.broadcasted_iota(
        jnp.int32, (tokens, tokens), 1
    )
    count = jnp.dot(
        chosen.astype(jnp.bfloat16),
        jnp.where(upto, 1.0, 0.0).astype(jnp.bfloat16),
        preferred_element_type=jnp.float32,
    ).astype(jnp.int32)
    rank[...] = jnp.where(chosen == 1, count - 1, -1)

    slot = lax.broadcasted_iota(jnp.int32, (GRP, CAP, tokens), 1)

    def hits(g):
        rows = rank[pl.ds(pl.multiple_of(g * GRP, GRP), GRP), :]
        return rows[:, None, :] == slot

    def slab(j):
        return pl.ds(pl.multiple_of(j * CAP, CAP), CAP)

    def dispatch(j):
        return pltpu.make_async_remote_copy(
            src_ref=packed.at[slab(j)],
            dst_ref=recv.at[slab(j)],
            send_sem=out_send.at[j],
            recv_sem=out_recv.at[j],
            device_id=peer(blk, seq, j, 1),
            device_id_type=MESH,
        )

    def give_back(j):
        return pltpu.make_async_remote_copy(
            src_ref=sent.at[slab(j)],
            dst_ref=ret.at[slab(j)],
            send_sem=back_send.at[j],
            recv_sem=back_recv.at[j],
            device_id=peer(blk, seq, j, -1),
            device_id_type=MESH,
        )

    def pack(g):
        one_hot = jnp.where(hits(g), 1.0, 0.0).reshape(ROWS, tokens).astype(jnp.bfloat16)
        rows = pl.ds(pl.multiple_of(g * ROWS, ROWS), ROWS)

        @pl.loop(0, normed.shape[1] // 512)
        def _(n):
            cols = pl.ds(pl.multiple_of(n * 512, 512), 512)
            packed[rows, cols] = jnp.dot(
                one_hot, normed[:, cols], preferred_element_type=jnp.float32
            ).astype(jnp.bfloat16)

    pack(0)
    recv[0:CAP, :] = packed[0:CAP, :]

    for g in range(NGRP):
        if g > 0:
            pack(g)
        lax.fori_loop(max(g * GRP, 1), (g + 1) * GRP, lambda j, _: (dispatch(j).start(), 0)[1], 0)

    logits = jnp.dot(normed[...], router_ref[...], preferred_element_type=jnp.float32)
    by_expert = jax.nn.sigmoid(logits).astype(jnp.bfloat16)
    order = jnp.where(
        expert == lax.broadcasted_iota(jnp.int32, (NPOS, NPOS), 1), 1.0, 0.0
    ).astype(jnp.bfloat16)
    gates[...] = lax.dot_general(
        order, by_expert, (((1,), (1,)), ((), ())), preferred_element_type=jnp.float32
    )

    load_gate_up.wait()
    load_down.wait()
    ff = down.shape[0]

    @pl.loop(0, NGRP)
    def _(g):
        first = jnp.where(g == 0, 1, g * GRP)
        lax.fori_loop(first, (g + 1) * GRP, lambda j, _: (dispatch(j).wait_recv(), 0)[1], 0)
        rows = pl.ds(pl.multiple_of(g * ROWS, ROWS), ROWS)

        @pl.loop(0, ff // TILE)
        def _(f):
            cols = pl.ds(pl.multiple_of(f * TILE, TILE), TILE)
            up_cols = pl.ds(pl.multiple_of(ff + f * TILE, TILE), TILE)
            gate = jnp.dot(recv[rows, :], gate_up[:, cols], preferred_element_type=jnp.float32)
            up = jnp.dot(recv[rows, :], gate_up[:, up_cols], preferred_element_type=jnp.float32)
            hidden[:, cols] = (jax.nn.silu(gate) * up).astype(jnp.bfloat16)

        @pl.loop(0, width // TILE)
        def _(n):
            cols = pl.ds(pl.multiple_of(n * TILE, TILE), TILE)
            sent[rows, cols] = jnp.dot(
                hidden[...], down[:, cols], preferred_element_type=jnp.float32
            ).astype(jnp.bfloat16)

        lax.fori_loop(first, (g + 1) * GRP, lambda j, _: (give_back(j).start(), 0)[1], 0)

    ret[0:CAP, :] = sent[0:CAP, :]
    total[...] = resid[...].astype(jnp.float32)

    @pl.loop(0, NGRP)
    def _(g):
        first = jnp.where(g == 0, 1, g * GRP)
        weight = gates[pl.ds(pl.multiple_of(g * GRP, GRP), GRP), :]
        spread = jnp.where(hits(g), weight[:, None, :], 0.0).reshape(ROWS, tokens)
        spread = spread.T.astype(jnp.bfloat16)
        lax.fori_loop(first, (g + 1) * GRP, lambda j, _: (give_back(j).wait_recv(), 0)[1], 0)
        rows = pl.ds(pl.multiple_of(g * ROWS, ROWS), ROWS)

        @pl.loop(0, width // 512)
        def _(n):
            cols = pl.ds(pl.multiple_of(n * 512, 512), 512)
            total[:, cols] += jnp.dot(spread, ret[rows, cols], preferred_element_type=jnp.float32)

    out_ref[...] = total[...].astype(jnp.bfloat16)

    def drain(j, _):
        page_arrival(j).wait_recv()
        page_copy(j).wait_send()
        dispatch(j).wait_send()
        give_back(j).wait_send()
        return 0

    lax.fori_loop(1, NPOS, drain, 0)
    own_page.wait()
    for n in range(width // SPAN):
        near_copy(0, n).wait_send()
        near_copy(1, n).wait_send()
        far_copy(n).wait_send()


def on_device(
    residual_in,
    segment_ids,
    attn_gain,
    w_qkv,
    w_out,
    ffn_gain,
    w_router,
    routes,
    w_gate_up,
    w_down,
    page_owner,
):
    tokens, width = residual_in.shape[1:]
    heads = w_qkv.shape[1]
    length = segment_ids.shape[1]
    page = length // NPOS
    ff = w_down.shape[1]
    slots = NPOS * CAP
    vmem = pl.BlockSpec(memory_space=pltpu.VMEM)
    hbm = pl.BlockSpec(memory_space=pl.ANY)
    dma = pltpu.SemaphoreType.DMA
    bf16 = jnp.bfloat16
    spans = width // SPAN
    residual_out, kv_cache = pl.pallas_call(
        layer_kernel,
        out_shape=(
            jax.ShapeDtypeStruct((tokens, width), bf16),
            jax.ShapeDtypeStruct((NPOS, page, heads * 2 * HEAD), bf16),
        ),
        in_specs=[vmem] * 7 + [hbm] * 4,
        out_specs=(vmem, vmem),
        scratch_shapes=[
            pltpu.VMEM((length, heads * HEAD), bf16),
            pltpu.VMEM((length, heads * 2 * HEAD), bf16),
            pltpu.VMEM((NPOS, page, heads * 2 * HEAD), bf16),
            pltpu.VMEM((length, heads * HEAD), bf16),
            pltpu.VMEM((2 * tokens, width), jnp.float32),
            pltpu.VMEM((2, tokens, width), bf16),
            pltpu.VMEM((2, tokens, width), bf16),
            pltpu.VMEM((tokens, width), bf16),
            pltpu.VMEM((tokens, width), bf16),
            pltpu.VMEM((tokens, width), bf16),
            pltpu.VMEM((tokens, width), bf16),
            pltpu.VMEM((NPOS, tokens), jnp.int32),
            pltpu.VMEM((NPOS, tokens), jnp.float32),
            pltpu.VMEM((slots, width), bf16),
            pltpu.VMEM((slots, width), bf16),
            pltpu.VMEM((max(slots, width), width), bf16),
            pltpu.VMEM((slots, width), bf16),
            pltpu.VMEM((ROWS, ff), bf16),
            pltpu.VMEM((width, 2 * ff), bf16),
            pltpu.VMEM((ff, width), bf16),
            pltpu.VMEM((tokens, width), jnp.float32),
            dma((4,)),
            dma,
            dma((NPOS,)),
            dma((NPOS,)),
            dma((NPOS,)),
            dma((NPOS,)),
            dma((NPOS,)),
            dma((NPOS,)),
            dma((2,)),
            dma((PARTS,)),
            dma((PARTS,)),
            dma((PARTS,)),
            dma((PARTS,)),
            dma((2, spans)),
            dma((2, spans)),
            dma((spans,)),
            dma((spans,)),
        ],
        compiler_params=pltpu.CompilerParams(
            collective_id=0, has_side_effects=True, vmem_limit_bytes=60 << 20
        ),
    )(
        residual_in[0],
        segment_ids,
        jnp.repeat(page_owner, page, axis=1),
        attn_gain.reshape(1, width),
        ffn_gain.reshape(1, width),
        w_router,
        routes[0].T,
        w_qkv.reshape(width, heads * 3 * HEAD),
        w_out.reshape(heads * HEAD, width),
        w_gate_up[0],
        w_down[0],
    )
    return (residual_out[None], kv_cache[None])


def solution(mesh):
    in_specs = (
        P("blk", "seq", None),
        P("blk", None),
        P(),
        P(None, "seq", None),
        P("seq", None, None),
        P(),
        P(),
        P("blk", "seq", None),
        P("blk", None, None),
        P("blk", None, None),
        P("blk", None),
    )
    out_specs = (P("blk", "seq", None), P("blk", None, None, "seq"))
    return jax.shard_map(
        on_device, mesh=mesh, in_specs=in_specs, out_specs=out_specs, check_vma=False
    )
```

time: 319 us -> 260 us (0.82)
  the two profiles are of different devices: /device:TPU:35 before, /device:TPU:81 now
where the time goes in v2:
time: 260 us
  Pallas kernels  242 us (93%)
  local copies, waits for them, and re-layouts  16.7 us (6%)
    pallas_call x1, Pallas kernels, on_device(): pl.pallas_call(layer_kernel, out_shape=(jax.ShapeDtypeStruct((tokens, wid...  242 us
    unnamed x4, local copies, waits for them, and re-layouts  12.7 us

profile of v2, /device:TPU:81, one launch (start us, length us, event | category | flops | bytes accessed | tf_op | source)
XLA Modules:
  0.0 259.6 jit_solution(254876932694025693)
XLA Ops:
  0.6 1.3 reshape.21.attn_gain_ref
  1.9 1.3 reshape.22.ffn_gain_ref
  3.2 0.7 broadcast_in_dim.11
  3.9 0.7 broadcast_in_dim.12.owner_ref
  4.6 1.9 copy.14.router_ref
  6.5 6.6 %copy.15 = bf16[256,8,4,384]{3,1,2,0:T(8,128)(2,1)} copy(bf16[256,8,4,384]{3,2,1,0:T(4,128)(2,1)} %bitcast.14) | data formatting | bytes 12582912
  13.1 242.3 %shard_map.125 = (bf16[128,2048]{1,0:T(8,128)(2,1)}, bf16[32,16,1024]{2,1,0:T(8,128)(2,1)}) custom-call(bf16[128,2048]{1,0:T(8,128)(2,1)} %bitcast.18, s32[1,512]{1,0:T(1,128)} %segment_ref.1, s32[1,512]{1,0:T(1,128)} %broadcast_in_dim.12.owner_ref, bf16[1,2048]{1,0:T(2,128)(2,1)} %reshape.21.attn_gain_ref, bf16[1,2048]{1,0:T(2,128)(2,1)} %reshape.22.ffn_gain_ref, ...), custom_call_target="tpu_custom_call" | custom-call | tf_op jit(solution)/shard_map/pallas_call | solution.py:508
  255.5 1.9 copy.18
  257.3 2.3 copy.19

commit v3 on v2

--- a/solution.py
+++ b/solution.py
@@ -10,9 +10,9 @@
 EPS = 1e-06
 NPOS = 32
 CAP = 48
-GRP = 8
-NGRP = NPOS // GRP
-ROWS = GRP * CAP
+SUB = 16
+NGRP = CAP // SUB
+ROWS = NPOS * SUB
 TILE = 256
 HEAD = 128
 PARTS = 4
@@ -20,20 +20,26 @@
 MESH = pl.DeviceIdType.MESH
 
 
-def step_of(position):
+def step_of(position, core):
     k = lax.rem(position * 3, NPOS)
     dx, dz, dy = lax.div(k, 16), lax.rem(lax.div(k, 4), 4), lax.rem(k, 4)
-    return dx, dz, dy
-
-
-def peer(blk, seq, position, sign, swap=True):
-    dx, dz, dy = step_of(position)
+    return dx, dz + core * (dy - dz), dy + core * (dz - dy)
+
+
+def place_at(blk, position, core, sign):
+    dx, dz, dy = step_of(position, core)
     x, z, y = lax.div(blk, 16), lax.rem(lax.div(blk, 4), 4), lax.rem(blk, 4)
     x = lax.rem(x + dx, 2)
     z = lax.rem(z + 4 + sign * dz, 4)
     y = lax.rem(y + 4 + sign * dy, 4)
-    other = 2 * dx * (1 - lax.rem(dy + dz, 2)) if swap else 0
-    return lax.rem(seq + other, 4), (x * 4 + z) * 4 + y
+    return (x * 4 + z) * 4 + y
+
+
+def peer(blk, seq, position, sign):
+    core = lax.rem(seq, 2)
+    dx, dz, dy = step_of(position, core)
+    other = 2 * dx * (1 - lax.rem(dy + dz, 2))
+    return lax.rem(seq + other, 4), place_at(blk, position, core, sign)
 
 
 def layer_kernel(
@@ -138,7 +144,7 @@
 
     def norm(wide, gain_ref):
         scale = lax.rsqrt(jnp.mean(wide * wide, axis=-1, keepdims=True) + EPS)
-        return (wide * scale * gain_ref[...].astype(jnp.float32)).astype(jnp.bfloat16)
+        return (wide * scale * gain_ref[...].astype(jnp.float32).reshape(1, width)).astype(jnp.bfloat16)
 
     def send(src, dst, send_sem, recv_sem, to):
         return pltpu.make_async_remote_copy(
@@ -205,6 +211,28 @@
                 [both[:, HEAD : 3 * HEAD], both[:, 4 * HEAD :]], axis=1
             )
 
+    tokens = tok
+    expert = place_at(blk, lax.broadcasted_iota(jnp.int32, (NPOS, 1), 0), core, 1)
+    chosen = jnp.zeros((NPOS, tokens), jnp.int32)
+    for k in range(routes_ref.shape[0]):
+        chosen = jnp.where(routes_ref[k : k + 1, :] == expert, 1, chosen)
+    upto = lax.broadcasted_iota(jnp.int32, (tokens, tokens), 0) <= lax.broadcasted_iota(
+        jnp.int32, (tokens, tokens), 1
+    )
+    count = jnp.dot(
+        chosen.astype(jnp.bfloat16),
+        jnp.where(upto, 1.0, 0.0).astype(jnp.bfloat16),
+        preferred_element_type=jnp.float32,
+    ).astype(jnp.int32)
+    rank[...] = jnp.where(chosen == 1, count - 1, -1)
+    slot = lax.broadcasted_iota(jnp.int32, (NPOS, SUB, tokens), 1)
+
+    def hits(g):
+        return rank[...][:, None, :] == slot + g * SUB
+
+    segment_row = segment_ref[...]
+    segment_column = jnp.broadcast_to(segment_row, (HEAD, length)).T
+
     load_qkv.wait()
     load_out.wait()
     load_gate_up.start()
@@ -219,48 +247,26 @@
     project(1 - half)
 
     def page_copy(j):
-        to_seq, to_blk = peer(blk, seq, j, 1, swap=False)
+        to_blk = place_at(blk, j, core, 1)
         return pltpu.make_async_remote_copy(
             src_ref=pages_ref.at[to_blk],
             dst_ref=kv_ref.at[blk],
             send_sem=kv_send.at[j],
             recv_sem=kv_recv.at[j],
-            device_id=(to_seq, to_blk),
+            device_id=(seq, to_blk),
             device_id_type=MESH,
         )
 
     def page_arrival(j):
-        to_seq, from_blk = peer(blk, seq, j, -1, swap=False)
+        from_blk = place_at(blk, j, core, -1)
         return pltpu.make_async_remote_copy(
             src_ref=pages_ref.at[from_blk],
             dst_ref=kv_ref.at[from_blk],
             send_sem=kv_send.at[j],
             recv_sem=kv_recv.at[j],
-            device_id=(to_seq, from_blk),
+            device_id=(seq, from_blk),
             device_id_type=MESH,
         )
-
-    page = length // NPOS
-    to_row = lax.broadcasted_iota(jnp.int32, (length, length), 0)
-    from_row = lax.broadcasted_iota(jnp.int32, (length, length), 1)
-    moves = (lax.rem(to_row, page) == lax.rem(from_row, page)) & (
-        lax.div(to_row, page) == owner_ref[...]
-    )
-    pages_ref[...] = (
-        jnp.dot(
-            jnp.where(moves, 1.0, 0.0).astype(jnp.bfloat16),
-            keys_values[...],
-            preferred_element_type=jnp.float32,
-        )
-        .astype(jnp.bfloat16)
-        .reshape(pages_ref.shape)
-    )
-    own_page = pltpu.make_async_copy(pages_ref.at[blk], kv_ref.at[blk], kv_local_sem)
-    own_page.start()
-    lax.fori_loop(1, NPOS, lambda j, _: (page_copy(j).start(), 0)[1], 0)
-
-    segment_row = segment_ref[...]
-    segment_column = jnp.broadcast_to(segment_row, (HEAD, length)).T
 
     def attend(index):
         rows = two_blocks(index)
@@ -331,6 +337,33 @@
         far_copy(n).start()
     attend(half)
     mix(1, half)
+    page = length // NPOS
+    spread_owner = lax.div(
+        lax.broadcasted_iota(jnp.int32, (NPOS, length), 1), page
+    ) == lax.broadcasted_iota(jnp.int32, (NPOS, length), 0)
+    owners = jnp.dot(
+        jnp.broadcast_to(owner_ref[...], (8, NPOS)).astype(jnp.bfloat16),
+        jnp.where(spread_owner, 1.0, 0.0).astype(jnp.bfloat16),
+        preferred_element_type=jnp.float32,
+    ).astype(jnp.int32)[0:1]
+    to_row = lax.broadcasted_iota(jnp.int32, (length, length), 0)
+    from_row = lax.broadcasted_iota(jnp.int32, (length, length), 1)
+    moves = (lax.rem(to_row, page) == lax.rem(from_row, page)) & (
+        lax.div(to_row, page) == owners
+    )
+    pages_ref[...] = (
+        jnp.dot(
+            jnp.where(moves, 1.0, 0.0).astype(jnp.bfloat16),
+            keys_values[...],
+            preferred_element_type=jnp.float32,
+        )
+        .astype(jnp.bfloat16)
+        .reshape(pages_ref.shape)
+    )
+    own_page = pltpu.make_async_copy(pages_ref.at[blk], kv_ref.at[blk], kv_local_sem)
+    own_page.start()
+    lax.fori_loop(1, NPOS, lambda j, _: (page_copy(j).start(), 0)[1], 0)
+
     for n in range(width // SPAN):
         mixed = reduced(1, n)
         far_copy(n).wait_recv()
@@ -344,51 +377,49 @@
         gather_out[i].wait_send()
         pass_out[i].wait_send()
 
-    tokens = tok
-    place = lax.broadcasted_iota(jnp.int32, (NPOS, 1), 0)
-    dx, dz, dy = step_of(place)
-    expert = lax.rem(lax.div(blk, 16) + dx, 2) * 16
-    expert = expert + lax.rem(lax.rem(lax.div(blk, 4), 4) + dz, 4) * 4
-    expert = expert + lax.rem(lax.rem(blk, 4) + dy, 4)
-    chosen = jnp.zeros((NPOS, tokens), jnp.int32)
-    for k in range(routes_ref.shape[0]):
-        chosen = jnp.where(routes_ref[k : k + 1, :] == expert, 1, chosen)
-    upto = lax.broadcasted_iota(jnp.int32, (tokens, tokens), 0) <= lax.broadcasted_iota(
-        jnp.int32, (tokens, tokens), 1
-    )
-    count = jnp.dot(
-        chosen.astype(jnp.bfloat16),
-        jnp.where(upto, 1.0, 0.0).astype(jnp.bfloat16),
-        preferred_element_type=jnp.float32,
-    ).astype(jnp.int32)
-    rank[...] = jnp.where(chosen == 1, count - 1, -1)
-
-    slot = lax.broadcasted_iota(jnp.int32, (GRP, CAP, tokens), 1)
-
-    def hits(g):
-        rows = rank[pl.ds(pl.multiple_of(g * GRP, GRP), GRP), :]
-        return rows[:, None, :] == slot
-
-    def slab(j):
-        return pl.ds(pl.multiple_of(j * CAP, CAP), CAP)
-
-    def dispatch(j):
+    def slab(g, j):
+        return pl.ds(pl.multiple_of(g * ROWS + j * SUB, SUB), SUB)
+
+    def others(g):
+        return pl.ds(pl.multiple_of(g * ROWS + SUB, SUB), ROWS - SUB)
+
+    def dispatch(g, j):
         return pltpu.make_async_remote_copy(
-            src_ref=packed.at[slab(j)],
-            dst_ref=recv.at[slab(j)],
-            send_sem=out_send.at[j],
-            recv_sem=out_recv.at[j],
+            src_ref=packed.at[slab(g, j)],
+            dst_ref=recv.at[slab(g, j)],
+            send_sem=out_send.at[g],
+            recv_sem=out_recv.at[g],
             device_id=peer(blk, seq, j, 1),
             device_id_type=MESH,
         )
 
-    def give_back(j):
+    def give_back(g, j):
         return pltpu.make_async_remote_copy(
-            src_ref=sent.at[slab(j)],
-            dst_ref=ret.at[slab(j)],
-            send_sem=back_send.at[j],
-            recv_sem=back_recv.at[j],
+            src_ref=sent.at[slab(g, j)],
+            dst_ref=ret.at[slab(g, j)],
+            send_sem=back_send.at[g],
+            recv_sem=back_recv.at[g],
             device_id=peer(blk, seq, j, -1),
+            device_id_type=MESH,
+        )
+
+    def dispatch_all(g):
+        return pltpu.make_async_remote_copy(
+            src_ref=packed.at[others(g)],
+            dst_ref=recv.at[others(g)],
+            send_sem=out_send.at[g],
+            recv_sem=out_recv.at[g],
+            device_id=(mate, blk),
+            device_id_type=MESH,
+        )
+
+    def give_back_all(g):
+        return pltpu.make_async_remote_copy(
+            src_ref=sent.at[others(g)],
+            dst_ref=ret.at[others(g)],
+            send_sem=back_send.at[g],
+            recv_sem=back_recv.at[g],
+            device_id=(mate, blk),
             device_id_type=MESH,
         )
 
@@ -403,21 +434,24 @@
                 one_hot, normed[:, cols], preferred_element_type=jnp.float32
             ).astype(jnp.bfloat16)
 
-    pack(0)
-    recv[0:CAP, :] = packed[0:CAP, :]
-
     for g in range(NGRP):
-        if g > 0:
-            pack(g)
-        lax.fori_loop(max(g * GRP, 1), (g + 1) * GRP, lambda j, _: (dispatch(j).start(), 0)[1], 0)
-
-    logits = jnp.dot(normed[...], router_ref[...], preferred_element_type=jnp.float32)
-    by_expert = jax.nn.sigmoid(logits).astype(jnp.bfloat16)
+        pack(g)
+        lax.fori_loop(1, NPOS, lambda j, _: (dispatch(g, j).start(), 0)[1], 0)
+        recv[slab(g, 0), :] = packed[slab(g, 0), :]
+
+    logits = lax.dot_general(
+        router_ref[...],
+        normed[...],
+        (((1,), (1,)), ((), ())),
+        preferred_element_type=jnp.float32,
+    )
     order = jnp.where(
         expert == lax.broadcasted_iota(jnp.int32, (NPOS, NPOS), 1), 1.0, 0.0
     ).astype(jnp.bfloat16)
-    gates[...] = lax.dot_general(
-        order, by_expert, (((1,), (1,)), ((), ())), preferred_element_type=jnp.float32
+    gates[...] = jnp.dot(
+        order,
+        jax.nn.sigmoid(logits).astype(jnp.bfloat16),
+        preferred_element_type=jnp.float32,
     )
 
     load_gate_up.wait()
@@ -426,8 +460,7 @@
 
     @pl.loop(0, NGRP)
     def _(g):
-        first = jnp.where(g == 0, 1, g * GRP)
-        lax.fori_loop(first, (g + 1) * GRP, lambda j, _: (dispatch(j).wait_recv(), 0)[1], 0)
+        dispatch_all(g).wait_recv()
         rows = pl.ds(pl.multiple_of(g * ROWS, ROWS), ROWS)
 
         @pl.loop(0, ff // TILE)
@@ -445,18 +478,16 @@
                 hidden[...], down[:, cols], preferred_element_type=jnp.float32
             ).astype(jnp.bfloat16)
 
-        lax.fori_loop(first, (g + 1) * GRP, lambda j, _: (give_back(j).start(), 0)[1], 0)
-
-    ret[0:CAP, :] = sent[0:CAP, :]
+        lax.fori_loop(1, NPOS, lambda j, _: (give_back(g, j).start(), 0)[1], 0)
+        ret[slab(g, 0), :] = sent[slab(g, 0), :]
+
     total[...] = resid[...].astype(jnp.float32)
 
     @pl.loop(0, NGRP)
     def _(g):
-        first = jnp.where(g == 0, 1, g * GRP)
-        weight = gates[pl.ds(pl.multiple_of(g * GRP, GRP), GRP), :]
-        spread = jnp.where(hits(g), weight[:, None, :], 0.0).reshape(ROWS, tokens)
+        spread = jnp.where(hits(g), gates[...][:, None, :], 0.0).reshape(ROWS, tokens)
         spread = spread.T.astype(jnp.bfloat16)
-        lax.fori_loop(first, (g + 1) * GRP, lambda j, _: (give_back(j).wait_recv(), 0)[1], 0)
+        give_back_all(g).wait_recv()
         rows = pl.ds(pl.multiple_of(g * ROWS, ROWS), ROWS)
 
         @pl.loop(0, width // 512)
@@ -469,11 +500,12 @@
     def drain(j, _):
         page_arrival(j).wait_recv()
         page_copy(j).wait_send()
-        dispatch(j).wait_send()
-        give_back(j).wait_send()
         return 0
 
     lax.fori_loop(1, NPOS, drain, 0)
+    for g in range(NGRP):
+        dispatch_all(g).wait_send()
+        give_back_all(g).wait_send()
     own_page.wait()
     for n in range(width // SPAN):
         near_copy(0, n).wait_send()
@@ -537,10 +569,10 @@
             pltpu.VMEM((tokens, width), jnp.float32),
             dma((4,)),
             dma,
-            dma((NPOS,)),
-            dma((NPOS,)),
-            dma((NPOS,)),
-            dma((NPOS,)),
+            dma((NGRP,)),
+            dma((NGRP,)),
+            dma((NGRP,)),
+            dma((NGRP,)),
             dma((NPOS,)),
             dma((NPOS,)),
             dma((2,)),
@@ -559,10 +591,10 @@
     )(
         residual_in[0],
         segment_ids,
-        jnp.repeat(page_owner, page, axis=1),
-        attn_gain.reshape(1, width),
-        ffn_gain.reshape(1, width),
-        w_router,
+        page_owner,
+        attn_gain,
+        ffn_gain,
+        w_router.T,
         routes[0].T,
         w_qkv.reshape(width, heads * 3 * HEAD),
         w_out.reshape(heads * HEAD, width),

time: 260 us -> 212 us (0.82)
  the two profiles are of different devices: /device:TPU:81 before, /device:TPU:0 now
where the time goes in v3:
time: 212 us; the launch traced here: 210 us
  Pallas kernels  199 us (94%)
  local copies, waits for them, and re-layouts  10.8 us (5%)
    pallas_call x1, Pallas kernels, on_device(): pl.pallas_call(layer_kernel, out_shape=(jax.ShapeDtypeStruct((tokens, wid...  199 us
    unnamed x3, local copies, waits for them, and re-layouts  10.8 us

profile of v3, /device:TPU:0, one launch (start us, length us, event | category | flops | bytes accessed | tf_op | source)
XLA Modules:
  0.0 210.4 jit_solution(675213423979826055)
XLA Ops:
  0.6 6.6 %copy.13 = bf16[256,8,4,384]{3,1,2,0:T(8,128)(2,1)} copy(bf16[256,8,4,384]{3,2,1,0:T(4,128)(2,1)} %bitcast.14) | data formatting | bytes 12582912
  7.2 199.0 %shard_map.122 = (bf16[128,2048]{1,0:T(8,128)(2,1)}, bf16[32,16,1024]{2,1,0:T(8,128)(2,1)}) custom-call(bf16[128,2048]{1,0:T(8,128)(2,1)} %bitcast.18, s32[1,512]{1,0:T(1,128)} %segment_ref.1, s32[1,32]{1,0:T(1,128)} %owner_ref.1, bf16[2048]{0:T(1024)(128)(2,1)} %attn_gain_ref.1, bf16[2048]{0:T(1024)(128)(2,1)} %ffn_gain_ref.1, bf16[32,2048]{1,0:T(8,128)(2,1)} %bitcast.20, ...), custom_call_target="tpu_custom_call" | custom-call | tf_op jit(solution)/shard_map/pallas_call | solution.py:540
  206.3 1.9 copy.16
  208.1 2.3 %copy.17 = bf16[1,32,16,1024]{3,2,1,0:T(8,128)(2,1)} copy(bf16[1,32,16,1024]{3,2,1,0:T(8,128)(2,1)} %bitcast.17) | data formatting | bytes 2097152

commit v4 on v3

--- a/solution.py
+++ b/solution.py
@@ -11,17 +11,20 @@
 NPOS = 32
 CAP = 48
 SUB = 16
-NGRP = CAP // SUB
-ROWS = NPOS * SUB
+RING = 4
+PLANE = 8
+ROWS = PLANE * CAP
+PIECE = 32
 TILE = 256
 HEAD = 128
 PARTS = 4
 SPAN = 512
 MESH = pl.DeviceIdType.MESH
+SHIFTS = (0, 1, 3, 2)
 
 
 def step_of(position, core):
-    k = lax.rem(position * 3, NPOS)
+    k = lax.rem(position * 11, NPOS)
     dx, dz, dy = lax.div(k, 16), lax.rem(lax.div(k, 4), 4), lax.rem(k, 4)
     return dx, dz + core * (dy - dz), dy + core * (dz - dy)
 
@@ -35,11 +38,32 @@
     return (x * 4 + z) * 4 + y
 
 
-def peer(blk, seq, position, sign):
+def locate(blk, core):
+    x, z, y = lax.div(blk, 16), lax.rem(lax.div(blk, 4), 4), lax.rem(blk, 4)
+    return x, z + core * (y - z), y + core * (z - y)
+
+
+def index_of(x, u, v, core):
+    z, y = u + core * (v - u), v + core * (u - v)
+    return (x * 4 + z) * 4 + y
+
+
+def along_ring(blk, core, shift):
+    x, u, v = locate(blk, core)
+    return index_of(x, lax.rem(u + 4 + shift, 4), v, core)
+
+
+def in_plane(blk, core, position, sign):
+    x, u, v = locate(blk, core)
+    dx, dv = lax.div(position, 4), lax.rem(position, 4)
+    return index_of(lax.rem(x + dx, 2), u, lax.rem(v + 4 + sign * dv, 4), core)
+
+
+def plane_peer(blk, seq, position, sign):
     core = lax.rem(seq, 2)
-    dx, dz, dy = step_of(position, core)
-    other = 2 * dx * (1 - lax.rem(dy + dz, 2))
-    return lax.rem(seq + other, 4), place_at(blk, position, core, sign)
+    dx, dv = lax.div(position, 4), lax.rem(position, 4)
+    other = 2 * dx * (1 - lax.rem(dv, 2))
+    return lax.rem(seq + other, 4), in_plane(blk, core, position, sign)
 
 
 def layer_kernel(
@@ -66,7 +90,10 @@
     far_send,
     far_recv,
     resid,
-    normed,
+    blocks,
+    routed,
+    sums_out,
+    sums_in,
     rank,
     gates,
     packed,
@@ -94,6 +121,12 @@
     near_recv_sems,
     far_send_sems,
     far_recv_sems,
+    route_send,
+    route_recv,
+    ring_send,
+    ring_recv,
+    sum_send,
+    sum_recv,
 ):
     blk = lax.axis_index("blk")
     seq = lax.axis_index("seq")
@@ -119,23 +152,21 @@
 
     def greet(j, _):
         pl.semaphore_signal(
-            barrier, inc=1, device_id=peer(blk, seq, j, 1), device_id_type=MESH
+            barrier,
+            inc=1,
+            device_id=(seq, place_at(blk, j, core, 1)),
+            device_id_type=MESH,
         )
         return 0
 
     lax.fori_loop(1, NPOS, greet, 0)
-
-    def greet_swapped(i, _):
-        z, y = lax.div(i, 2), lax.rem(i, 2) * 2 + lax.rem(lax.div(i, 2), 2)
-        there = (lax.rem(lax.div(blk, 16) + 1, 2)) * 16
-        there = there + lax.rem(lax.rem(lax.div(blk, 4), 4) + z, 4) * 4
-        there = there + lax.rem(lax.rem(blk, 4) + y, 4)
+    for crossing in (4, 6):
         pl.semaphore_signal(
-            barrier, inc=1, device_id=(seq, there), device_id_type=MESH
-        )
-        return 0
-
-    lax.fori_loop(0, 8, greet_swapped, 0)
+            barrier,
+            inc=1,
+            device_id=plane_peer(blk, seq, crossing, 1),
+            device_id_type=MESH,
+        )
     for other in (mate, far):
         pl.semaphore_signal(barrier, inc=1, device_id=(other, blk), device_id_type=MESH)
 
@@ -161,7 +192,18 @@
         return everyone.at[pl.ds(pl.multiple_of(index * tok + i * rows, rows), rows)]
 
     everyone[block(seq), :] = norm(rows_ref[...].astype(jnp.float32), attn_gain_ref)
-    pl.semaphore_wait(barrier, NPOS - 1 + 8 + 2)
+    pl.semaphore_wait(barrier, NPOS - 1 + 2 + 2)
+
+    def route_copy(g):
+        return pltpu.make_async_remote_copy(
+            src_ref=routes_ref,
+            dst_ref=routed.at[g],
+            send_sem=route_send.at[g],
+            recv_sem=route_recv.at[g],
+            device_id=(seq, along_ring(blk, core, SHIFTS[g])),
+            device_id_type=MESH,
+        )
+
 
     own_out = send(
         everyone.at[block(seq)], everyone.at[block(seq)], own_sems.at[0], own_sems.at[1], mate
@@ -189,6 +231,8 @@
     for copy in gather_out:
         copy.start()
     own_out.start()
+    for g in range(1, RING):
+        route_copy(g).start()
 
     def two_blocks(index):
         return pl.ds(pl.multiple_of(index * 2 * tok, 2 * tok), 2 * tok)
@@ -212,23 +256,29 @@
             )
 
     tokens = tok
-    expert = place_at(blk, lax.broadcasted_iota(jnp.int32, (NPOS, 1), 0), core, 1)
-    chosen = jnp.zeros((NPOS, tokens), jnp.int32)
-    for k in range(routes_ref.shape[0]):
-        chosen = jnp.where(routes_ref[k : k + 1, :] == expert, 1, chosen)
-    upto = lax.broadcasted_iota(jnp.int32, (tokens, tokens), 0) <= lax.broadcasted_iota(
-        jnp.int32, (tokens, tokens), 1
-    )
-    count = jnp.dot(
-        chosen.astype(jnp.bfloat16),
-        jnp.where(upto, 1.0, 0.0).astype(jnp.bfloat16),
-        preferred_element_type=jnp.float32,
-    ).astype(jnp.int32)
-    rank[...] = jnp.where(chosen == 1, count - 1, -1)
-    slot = lax.broadcasted_iota(jnp.int32, (NPOS, SUB, tokens), 1)
+    expert = in_plane(blk, core, lax.broadcasted_iota(jnp.int32, (PLANE, 1), 0), 1)
+    slot = lax.broadcasted_iota(jnp.int32, (PLANE, CAP, tokens), 1)
+
+    def rank_tokens():
+        upto = lax.broadcasted_iota(jnp.int32, (tokens, tokens), 0) <= lax.broadcasted_iota(
+            jnp.int32, (tokens, tokens), 1
+        )
+        for g in range(RING):
+            if g > 0:
+                route_copy(g).wait_recv()
+            chosen = jnp.zeros((PLANE, tokens), jnp.int32)
+            for k in range(routes_ref.shape[0]):
+                named = routes_ref[k : k + 1, :] if g == 0 else routed[g, k : k + 1, :]
+                chosen = jnp.where(named == expert, 1, chosen)
+            count = jnp.dot(
+                chosen.astype(jnp.bfloat16),
+                jnp.where(upto, 1.0, 0.0).astype(jnp.bfloat16),
+                preferred_element_type=jnp.float32,
+            ).astype(jnp.int32)
+            rank[g] = jnp.where(chosen == 1, count - 1, -1)
 
     def hits(g):
-        return rank[...][:, None, :] == slot + g * SUB
+        return rank[g][:, None, :] == slot
 
     segment_row = segment_ref[...]
     segment_column = jnp.broadcast_to(segment_row, (HEAD, length)).T
@@ -239,6 +289,7 @@
     load_down.start()
     own_in.wait_recv()
     project(half)
+    rank_tokens()
     for i in range(PARTS):
         gather_in[i].wait_recv()
         pass_out[i].start()
@@ -371,35 +422,85 @@
         resid[:, column(n)] = (rows_ref[:, column(n)].astype(jnp.float32) + mixed).astype(
             jnp.bfloat16
         )
-    normed[...] = norm(resid[...].astype(jnp.float32), ffn_gain_ref)
+    blocks[0:tokens, :] = norm(resid[...].astype(jnp.float32), ffn_gain_ref)
     own_out.wait_send()
     for i in range(PARTS):
         gather_out[i].wait_send()
         pass_out[i].wait_send()
 
-    def slab(g, j):
-        return pl.ds(pl.multiple_of(g * ROWS + j * SUB, SUB), SUB)
+    def ring_piece(g, i):
+        rows = pl.ds(pl.multiple_of(i * PIECE, PIECE), PIECE)
+        to_rows = pl.ds(pl.multiple_of(g * tokens + i * PIECE, PIECE), PIECE)
+        return pltpu.make_async_remote_copy(
+            src_ref=blocks.at[rows],
+            dst_ref=blocks.at[to_rows],
+            send_sem=ring_send.at[g],
+            recv_sem=ring_recv.at[g],
+            device_id=(seq, along_ring(blk, core, SHIFTS[g])),
+            device_id_type=MESH,
+        )
+
+    def ring_all(g):
+        return pltpu.make_async_remote_copy(
+            src_ref=blocks.at[0:tokens],
+            dst_ref=blocks.at[pl.ds(g * tokens, tokens)],
+            send_sem=ring_send.at[g],
+            recv_sem=ring_recv.at[g],
+            device_id=(mate, blk),
+            device_id_type=MESH,
+        )
+
+    def sum_piece(g, i):
+        rows = pl.ds(pl.multiple_of(i * PIECE, PIECE), PIECE)
+        return pltpu.make_async_remote_copy(
+            src_ref=sums_out.at[g - 1, rows],
+            dst_ref=sums_in.at[g - 1, rows],
+            send_sem=sum_send.at[g],
+            recv_sem=sum_recv.at[g],
+            device_id=(seq, along_ring(blk, core, -SHIFTS[g])),
+            device_id_type=MESH,
+        )
+
+    def sum_all(g):
+        return pltpu.make_async_remote_copy(
+            src_ref=sums_out.at[g - 1],
+            dst_ref=sums_in.at[g - 1],
+            send_sem=sum_send.at[g],
+            recv_sem=sum_recv.at[g],
+            device_id=(mate, blk),
+            device_id_type=MESH,
+        )
+
+    def slab(g, p):
+        return pl.ds(pl.multiple_of(g * ROWS + p * CAP, SUB), CAP)
 
     def others(g):
-        return pl.ds(pl.multiple_of(g * ROWS + SUB, SUB), ROWS - SUB)
-
-    def dispatch(g, j):
-        return pltpu.make_async_remote_copy(
-            src_ref=packed.at[slab(g, j)],
-            dst_ref=recv.at[slab(g, j)],
+        return pl.ds(pl.multiple_of(g * ROWS + CAP, SUB), ROWS - CAP)
+
+    def nth(g, i):
+        p = lax.rem((lax.rem(i, PLANE - 1) + 1) * 3, PLANE)
+        start = g * ROWS + p * CAP + lax.div(i, PLANE - 1) * SUB
+        return p, pl.ds(pl.multiple_of(start, SUB), SUB)
+
+    def dispatch(g, i):
+        p, rows = nth(g, i)
+        return pltpu.make_async_remote_copy(
+            src_ref=packed.at[rows],
+            dst_ref=recv.at[rows],
             send_sem=out_send.at[g],
             recv_sem=out_recv.at[g],
-            device_id=peer(blk, seq, j, 1),
-            device_id_type=MESH,
-        )
-
-    def give_back(g, j):
-        return pltpu.make_async_remote_copy(
-            src_ref=sent.at[slab(g, j)],
-            dst_ref=ret.at[slab(g, j)],
+            device_id=plane_peer(blk, seq, p, 1),
+            device_id_type=MESH,
+        )
+
+    def give_back(g, i):
+        p, rows = nth(g, i)
+        return pltpu.make_async_remote_copy(
+            src_ref=sent.at[rows],
+            dst_ref=ret.at[rows],
             send_sem=back_send.at[g],
             recv_sem=back_recv.at[g],
-            device_id=peer(blk, seq, j, -1),
+            device_id=plane_peer(blk, seq, p, -1),
             device_id_type=MESH,
         )
 
@@ -425,40 +526,49 @@
 
     def pack(g):
         one_hot = jnp.where(hits(g), 1.0, 0.0).reshape(ROWS, tokens).astype(jnp.bfloat16)
-        rows = pl.ds(pl.multiple_of(g * ROWS, ROWS), ROWS)
-
-        @pl.loop(0, normed.shape[1] // 512)
+        rows = pl.ds(g * ROWS, ROWS)
+
+        @pl.loop(0, width // 512)
         def _(n):
             cols = pl.ds(pl.multiple_of(n * 512, 512), 512)
             packed[rows, cols] = jnp.dot(
-                one_hot, normed[:, cols], preferred_element_type=jnp.float32
+                one_hot,
+                blocks[g * tokens : (g + 1) * tokens, cols],
+                preferred_element_type=jnp.float32,
             ).astype(jnp.bfloat16)
 
-    for g in range(NGRP):
+    copies = (PLANE - 1) * (CAP // SUB)
+    pieces = tokens // PIECE
+    for g in range(1, RING):
+        lax.fori_loop(0, pieces, lambda i, _: (ring_piece(g, i).start(), 0)[1], 0)
+    for g in range(RING):
+        if g > 0:
+            ring_all(g).wait_recv()
         pack(g)
-        lax.fori_loop(1, NPOS, lambda j, _: (dispatch(g, j).start(), 0)[1], 0)
+        lax.fori_loop(0, copies, lambda i, _: (dispatch(g, i).start(), 0)[1], 0)
         recv[slab(g, 0), :] = packed[slab(g, 0), :]
 
-    logits = lax.dot_general(
-        router_ref[...],
-        normed[...],
-        (((1,), (1,)), ((), ())),
-        preferred_element_type=jnp.float32,
-    )
     order = jnp.where(
-        expert == lax.broadcasted_iota(jnp.int32, (NPOS, NPOS), 1), 1.0, 0.0
+        expert == lax.broadcasted_iota(jnp.int32, (PLANE, NPOS), 1), 1.0, 0.0
     ).astype(jnp.bfloat16)
-    gates[...] = jnp.dot(
-        order,
-        jax.nn.sigmoid(logits).astype(jnp.bfloat16),
-        preferred_element_type=jnp.float32,
-    )
+    for g in range(RING):
+        logits = lax.dot_general(
+            router_ref[...],
+            blocks[g * tokens : (g + 1) * tokens, :],
+            (((1,), (1,)), ((), ())),
+            preferred_element_type=jnp.float32,
+        )
+        gates[g] = jnp.dot(
+            order,
+            jax.nn.sigmoid(logits).astype(jnp.bfloat16),
+            preferred_element_type=jnp.float32,
+        )
 
     load_gate_up.wait()
     load_down.wait()
     ff = down.shape[0]
 
-    @pl.loop(0, NGRP)
+    @pl.loop(0, RING)
     def _(g):
         dispatch_all(g).wait_recv()
         rows = pl.ds(pl.multiple_of(g * ROWS, ROWS), ROWS)
@@ -478,24 +588,38 @@
                 hidden[...], down[:, cols], preferred_element_type=jnp.float32
             ).astype(jnp.bfloat16)
 
-        lax.fori_loop(1, NPOS, lambda j, _: (give_back(g, j).start(), 0)[1], 0)
+        lax.fori_loop(0, copies, lambda i, _: (give_back(g, i).start(), 0)[1], 0)
         ret[slab(g, 0), :] = sent[slab(g, 0), :]
 
-    total[...] = resid[...].astype(jnp.float32)
-
-    @pl.loop(0, NGRP)
-    def _(g):
-        spread = jnp.where(hits(g), gates[...][:, None, :], 0.0).reshape(ROWS, tokens)
+    for g in range(RING):
+        spread = jnp.where(hits(g), gates[g][:, None, :], 0.0).reshape(ROWS, tokens)
         spread = spread.T.astype(jnp.bfloat16)
         give_back_all(g).wait_recv()
-        rows = pl.ds(pl.multiple_of(g * ROWS, ROWS), ROWS)
 
         @pl.loop(0, width // 512)
         def _(n):
             cols = pl.ds(pl.multiple_of(n * 512, 512), 512)
-            total[:, cols] += jnp.dot(spread, ret[rows, cols], preferred_element_type=jnp.float32)
-
-    out_ref[...] = total[...].astype(jnp.bfloat16)
+            mixture = jnp.dot(
+                spread,
+                ret[g * ROWS : (g + 1) * ROWS, cols],
+                preferred_element_type=jnp.float32,
+            )
+            if g == 0:
+                total[:, cols] = resid[:, cols].astype(jnp.float32) + mixture
+            else:
+                sums_out[g - 1, :, cols] = mixture.astype(jnp.bfloat16)
+
+        if g > 0:
+            lax.fori_loop(0, pieces, lambda i, _: (sum_piece(g, i).start(), 0)[1], 0)
+
+    for g in range(1, RING):
+        sum_all(g).wait_recv()
+        if g < RING - 1:
+            total[...] += sums_in[g - 1].astype(jnp.float32)
+        else:
+            out_ref[...] = (total[...] + sums_in[g - 1].astype(jnp.float32)).astype(
+                jnp.bfloat16
+            )
 
     def drain(j, _):
         page_arrival(j).wait_recv()
@@ -503,9 +627,13 @@
         return 0
 
     lax.fori_loop(1, NPOS, drain, 0)
-    for g in range(NGRP):
+    for g in range(RING):
         dispatch_all(g).wait_send()
         give_back_all(g).wait_send()
+        if g > 0:
+            route_copy(g).wait_send()
+            ring_all(g).wait_send()
+            sum_all(g).wait_send()
     own_page.wait()
     for n in range(width // SPAN):
         near_copy(0, n).wait_send()
@@ -544,7 +672,7 @@
             jax.ShapeDtypeStruct((NPOS, page, heads * 2 * HEAD), bf16),
         ),
         in_specs=[vmem] * 7 + [hbm] * 4,
-        out_specs=(vmem, vmem),
+        out_specs=(vmem, hbm),
         scratch_shapes=[
             pltpu.VMEM((length, heads * HEAD), bf16),
             pltpu.VMEM((length, heads * 2 * HEAD), bf16),
@@ -556,9 +684,12 @@
             pltpu.VMEM((tokens, width), bf16),
             pltpu.VMEM((tokens, width), bf16),
             pltpu.VMEM((tokens, width), bf16),
-            pltpu.VMEM((tokens, width), bf16),
-            pltpu.VMEM((NPOS, tokens), jnp.int32),
-            pltpu.VMEM((NPOS, tokens), jnp.float32),
+            pltpu.VMEM((RING * tokens, width), bf16),
+            pltpu.VMEM((RING,) + routes.shape[2:] + (tokens,), jnp.int32),
+            pltpu.VMEM((RING - 1, tokens, width), bf16),
+            pltpu.VMEM((RING - 1, tokens, width), bf16),
+            pltpu.VMEM((RING, PLANE, tokens), jnp.int32),
+            pltpu.VMEM((RING, PLANE, tokens), jnp.float32),
             pltpu.VMEM((slots, width), bf16),
             pltpu.VMEM((slots, width), bf16),
             pltpu.VMEM((max(slots, width), width), bf16),
@@ -569,10 +700,10 @@
             pltpu.VMEM((tokens, width), jnp.float32),
             dma((4,)),
             dma,
-            dma((NGRP,)),
-            dma((NGRP,)),
-            dma((NGRP,)),
-            dma((NGRP,)),
+            dma((RING,)),
+            dma((RING,)),
+            dma((RING,)),
+            dma((RING,)),
             dma((NPOS,)),
             dma((NPOS,)),
             dma((2,)),
@@ -584,6 +715,12 @@
             dma((2, spans)),
             dma((spans,)),
             dma((spans,)),
+            dma((RING,)),
+            dma((RING,)),
+            dma((RING,)),
+            dma((RING,)),
+            dma((RING,)),
+            dma((RING,)),
         ],
         compiler_params=pltpu.CompilerParams(
             collective_id=0, has_side_effects=True, vmem_limit_bytes=60 << 20

time: 212 us -> 166 us (0.78)
  the two profiles are of different devices: /device:TPU:0 before, /device:TPU:104 now
where the time goes in v4:
time: 166 us
  Pallas kernels  154 us (93%)
  local copies, waits for them, and re-layouts  10.8 us (7%)
    pallas_call x1, Pallas kernels, on_device(): pl.pallas_call(layer_kernel, out_shape=(jax.ShapeDtypeStruct((tokens, wid...  154 us
    unnamed x3, local copies, waits for them, and re-layouts  10.8 us

profile of v4, /device:TPU:104, one launch (start us, length us, event | category | flops | bytes accessed | tf_op | source)
XLA Modules:
  0.0 165.5 jit_solution(11335352911589453253)
XLA Ops:
  0.6 6.6 %copy.13 = bf16[256,8,4,384]{3,1,2,0:T(8,128)(2,1)} copy(bf16[256,8,4,384]{3,2,1,0:T(4,128)(2,1)} %bitcast.14) | data formatting | bytes 12582912
  7.2 154.1 %shard_map.122 = (bf16[128,2048]{1,0:T(8,128)(2,1)}, bf16[32,16,1024]{2,1,0:T(8,128)(2,1)}) custom-call(bf16[128,2048]{1,0:T(8,128)(2,1)} %bitcast.18, s32[1,512]{1,0:T(1,128)} %segment_ref.1, s32[1,32]{1,0:T(1,128)} %owner_ref.1, bf16[2048]{0:T(1024)(128)(2,1)} %attn_gain_ref.1, bf16[2048]{0:T(1024)(128)(2,1)} %ffn_gain_ref.1, bf16[32,2048]{1,0:T(8,128)(2,1)} %bitcast.20, ...), custom_call_target="tpu_custom_call" | custom-call | tf_op jit(solution)/shard_map/pallas_call | solution.py:668
  161.4 1.9 %copy.16 = bf16[1,128,2048]{2,1,0:T(8,128)(2,1)} copy(bf16[1,128,2048]{2,1,0:T(8,128)(2,1)} %bitcast.19) | data formatting | bytes 1048576
  163.2 2.3 %copy.17 = bf16[1,32,16,1024]{3,2,1,0:T(8,128)(2,1)} copy(bf16[1,32,16,1024]{3,2,1,0:T(8,128)(2,1)} %bitcast.17) | data formatting | bytes 2097152

commit v5 on v4

--- a/solution.py
+++ b/solution.py
@@ -15,12 +15,15 @@
 PLANE = 8
 ROWS = PLANE * CAP
 PIECE = 32
+LOAD = 256
+TURN = 64
 TILE = 256
 HEAD = 128
 PARTS = 4
 SPAN = 512
 MESH = pl.DeviceIdType.MESH
-SHIFTS = (0, 1, 3, 2)
+SHIFTS = (1, 3, 2, 0)
+OWN = RING - 1
 
 
 def step_of(position, core):
@@ -121,6 +124,8 @@
     near_recv_sems,
     far_send_sems,
     far_recv_sems,
+    staged,
+    stage_sems,
     route_send,
     route_recv,
     ring_send,
@@ -138,14 +143,22 @@
     width = rows_ref.shape[1]
     length = 4 * tok
     heads = out_hbm.shape[0] // HEAD
-    w_qkv = sent.at[0:width, 0 : qkv_hbm.shape[1]]
+    columns = qkv_hbm.shape[2]
+    w_qkv = sent.at[0:width, 0 : heads * columns]
     w_out = packed.at[0 : out_hbm.shape[0]]
     everyone = packed.at[out_hbm.shape[0] : out_hbm.shape[0] + length]
-    load_qkv = pltpu.make_async_copy(qkv_hbm, w_qkv, weight_sems.at[2])
+
+    def load_qkv(i):
+        rows = pl.ds(pl.multiple_of(i * LOAD, LOAD), LOAD)
+        return pltpu.make_async_copy(
+            qkv_hbm.at[rows], staged.at[lax.rem(i, 2)], stage_sems.at[lax.rem(i, 2)]
+        )
+
     load_out = pltpu.make_async_copy(out_hbm, w_out, weight_sems.at[3])
     load_gate_up = pltpu.make_async_copy(gate_up_hbm, gate_up, weight_sems.at[0])
     load_down = pltpu.make_async_copy(down_hbm, down, weight_sems.at[1])
-    load_qkv.start()
+    load_qkv(0).start()
+    load_qkv(1).start()
     load_out.start()
 
     barrier = pltpu.get_barrier_semaphore()
@@ -231,7 +244,7 @@
     for copy in gather_out:
         copy.start()
     own_out.start()
-    for g in range(1, RING):
+    for g in range(OWN):
         route_copy(g).start()
 
     def two_blocks(index):
@@ -259,16 +272,18 @@
     expert = in_plane(blk, core, lax.broadcasted_iota(jnp.int32, (PLANE, 1), 0), 1)
     slot = lax.broadcasted_iota(jnp.int32, (PLANE, CAP, tokens), 1)
 
+    own_rows = slice(OWN * tokens, RING * tokens)
+
     def rank_tokens():
         upto = lax.broadcasted_iota(jnp.int32, (tokens, tokens), 0) <= lax.broadcasted_iota(
             jnp.int32, (tokens, tokens), 1
         )
         for g in range(RING):
-            if g > 0:
+            if g != OWN:
                 route_copy(g).wait_recv()
             chosen = jnp.zeros((PLANE, tokens), jnp.int32)
             for k in range(routes_ref.shape[0]):
-                named = routes_ref[k : k + 1, :] if g == 0 else routed[g, k : k + 1, :]
+                named = routes_ref[k : k + 1, :] if g == OWN else routed[g, k : k + 1, :]
                 chosen = jnp.where(named == expert, 1, chosen)
             count = jnp.dot(
                 chosen.astype(jnp.bfloat16),
@@ -283,14 +298,33 @@
     segment_row = segment_ref[...]
     segment_column = jnp.broadcast_to(segment_row, (HEAD, length)).T
 
-    load_qkv.wait()
+    loads = width // LOAD
+
+    @pl.loop(0, loads)
+    def _(i):
+        load_qkv(i).wait()
+
+        @pl.loop(0, LOAD // TURN)
+        def _(t):
+            some = staged[lax.rem(i, 2), pl.ds(pl.multiple_of(t * TURN, TURN), TURN)]
+            rows = pl.ds(pl.multiple_of(i * LOAD + t * TURN, TURN), TURN)
+            for head in range(heads):
+                w_qkv[rows, head * columns : (head + 1) * columns] = some[:, head, :]
+
+        @pl.when(i < loads - 2)
+        def _():
+            load_qkv(i + 2).start()
+
     load_out.wait()
     load_gate_up.start()
     load_down.start()
     own_in.wait_recv()
+    for i in range(PARTS // 2):
+        gather_in[i].wait_recv()
+        pass_out[i].start()
     project(half)
     rank_tokens()
-    for i in range(PARTS):
+    for i in range(PARTS // 2, PARTS):
         gather_in[i].wait_recv()
         pass_out[i].start()
     for i in range(PARTS):
@@ -422,14 +456,14 @@
         resid[:, column(n)] = (rows_ref[:, column(n)].astype(jnp.float32) + mixed).astype(
             jnp.bfloat16
         )
-    blocks[0:tokens, :] = norm(resid[...].astype(jnp.float32), ffn_gain_ref)
+    blocks[own_rows, :] = norm(resid[...].astype(jnp.float32), ffn_gain_ref)
     own_out.wait_send()
     for i in range(PARTS):
         gather_out[i].wait_send()
         pass_out[i].wait_send()
 
     def ring_piece(g, i):
-        rows = pl.ds(pl.multiple_of(i * PIECE, PIECE), PIECE)
+        rows = pl.ds(pl.multiple_of(OWN * tokens + i * PIECE, PIECE), PIECE)
         to_rows = pl.ds(pl.multiple_of(g * tokens + i * PIECE, PIECE), PIECE)
         return pltpu.make_async_remote_copy(
             src_ref=blocks.at[rows],
@@ -442,7 +476,7 @@
 
     def ring_all(g):
         return pltpu.make_async_remote_copy(
-            src_ref=blocks.at[0:tokens],
+            src_ref=blocks.at[own_rows],
             dst_ref=blocks.at[pl.ds(g * tokens, tokens)],
             send_sem=ring_send.at[g],
             recv_sem=ring_recv.at[g],
@@ -453,8 +487,8 @@
     def sum_piece(g, i):
         rows = pl.ds(pl.multiple_of(i * PIECE, PIECE), PIECE)
         return pltpu.make_async_remote_copy(
-            src_ref=sums_out.at[g - 1, rows],
-            dst_ref=sums_in.at[g - 1, rows],
+            src_ref=sums_out.at[g, rows],
+            dst_ref=sums_in.at[g, rows],
             send_sem=sum_send.at[g],
             recv_sem=sum_recv.at[g],
             device_id=(seq, along_ring(blk, core, -SHIFTS[g])),
@@ -463,8 +497,8 @@
 
     def sum_all(g):
         return pltpu.make_async_remote_copy(
-            src_ref=sums_out.at[g - 1],
-            dst_ref=sums_in.at[g - 1],
+            src_ref=sums_out.at[g],
+            dst_ref=sums_in.at[g],
             send_sem=sum_send.at[g],
             recv_sem=sum_recv.at[g],
             device_id=(mate, blk),
@@ -539,10 +573,10 @@
 
     copies = (PLANE - 1) * (CAP // SUB)
     pieces = tokens // PIECE
-    for g in range(1, RING):
+    for g in range(OWN):
         lax.fori_loop(0, pieces, lambda i, _: (ring_piece(g, i).start(), 0)[1], 0)
     for g in range(RING):
-        if g > 0:
+        if g != OWN:
             ring_all(g).wait_recv()
         pack(g)
         lax.fori_loop(0, copies, lambda i, _: (dispatch(g, i).start(), 0)[1], 0)
@@ -604,22 +638,20 @@
                 ret[g * ROWS : (g + 1) * ROWS, cols],
                 preferred_element_type=jnp.float32,
             )
-            if g == 0:
+            if g == OWN:
                 total[:, cols] = resid[:, cols].astype(jnp.float32) + mixture
             else:
-                sums_out[g - 1, :, cols] = mixture.astype(jnp.bfloat16)
-
-        if g > 0:
+                sums_out[g, :, cols] = mixture.astype(jnp.bfloat16)
+
+        if g != OWN:
             lax.fori_loop(0, pieces, lambda i, _: (sum_piece(g, i).start(), 0)[1], 0)
 
-    for g in range(1, RING):
+    for g in range(OWN):
         sum_all(g).wait_recv()
-        if g < RING - 1:
-            total[...] += sums_in[g - 1].astype(jnp.float32)
-        else:
-            out_ref[...] = (total[...] + sums_in[g - 1].astype(jnp.float32)).astype(
-                jnp.bfloat16
-            )
+    summed = total[...]
+    for g in range(OWN):
+        summed = summed + sums_in[g].astype(jnp.float32)
+    out_ref[...] = summed.astype(jnp.bfloat16)
 
     def drain(j, _):
         page_arrival(j).wait_recv()
@@ -630,7 +662,7 @@
     for g in range(RING):
         dispatch_all(g).wait_send()
         give_back_all(g).wait_send()
-        if g > 0:
+        if g != OWN:
             route_copy(g).wait_send()
             ring_all(g).wait_send()
             sum_all(g).wait_send()
@@ -715,6 +747,8 @@
             dma((2, spans)),
             dma((spans,)),
             dma((spans,)),
+            pltpu.VMEM((2, LOAD) + w_qkv.shape[1:], bf16),
+            dma((2,)),
             dma((RING,)),
             dma((RING,)),
             dma((RING,)),
@@ -733,7 +767,7 @@
         ffn_gain,
         w_router.T,
         routes[0].T,
-        w_qkv.reshape(width, heads * 3 * HEAD),
+        w_qkv,
         w_out.reshape(heads * HEAD, width),
         w_gate_up[0],
         w_down[0],

time: 166 us -> 155 us (0.934)
  the two profiles are of different devices: /device:TPU:104 before, /device:TPU:40 now
where the time goes in v5:
time: 155 us
  Pallas kernels  150 us (97%)
  local copies, waits for them, and re-layouts  4.19 us (3%)
    pallas_call x1, Pallas kernels, on_device(): pl.pallas_call(layer_kernel, out_shape=(jax.ShapeDtypeStruct((tokens, wid...  150 us
    unnamed x2, local copies, waits for them, and re-layouts  4.19 us

profile of v5, /device:TPU:40, one launch (start us, length us, event | category | flops | bytes accessed | tf_op | source)
XLA Modules:
  0.0 155.0 jit_solution(13013322190182762774)
XLA Ops:
  0.6 150.1 %shard_map.122 = (bf16[128,2048]{1,0:T(8,128)(2,1)}, bf16[32,16,1024]{2,1,0:T(8,128)(2,1)}) custom-call(bf16[128,2048]{1,0:T(8,128)(2,1)} %bitcast.14, s32[1,512]{1,0:T(1,128)} %segment_ref.1, s32[1,32]{1,0:T(1,128)} %owner_ref.1, bf16[2048]{0:T(1024)(128)(2,1)} %attn_gain_ref.1, bf16[2048]{0:T(1024)(128)(2,1)} %ffn_gain_ref.1, bf16[32,2048]{1,0:T(8,128)(2,1)} %bitcast.16, ...), custom_call_target="tpu_custom_call" | custom-call | tf_op jit(solution)/shard_map/pallas_call | solution.py:700
  150.8 1.9 %copy.15 = bf16[1,128,2048]{2,1,0:T(8,128)(2,1)} copy(bf16[1,128,2048]{2,1,0:T(8,128)(2,1)} %bitcast.15) | data formatting | bytes 1048576
  152.7 2.3 %copy.16 = bf16[1,32,16,1024]{3,2,1,0:T(8,128)(2,1)} copy(bf16[1,32,16,1024]{3,2,1,0:T(8,128)(2,1)} %bitcast.13) | data formatting | bytes 2097152

commit v6 on v5

--- a/solution.py
+++ b/solution.py
@@ -379,23 +379,28 @@
     def column(n):
         return pl.ds(n * SPAN, SPAN)
 
-    def near_copy(which, n):
+    def strip(r):
+        return pl.ds(r * PIECE, PIECE)
+
+    def near_copy(which, r):
         return send(
-            near_send.at[which, :, column(n)],
-            near_recv.at[which, :, column(n)],
-            near_send_sems.at[which, n],
-            near_recv_sems.at[which, n],
+            near_send.at[which, strip(r)],
+            near_recv.at[which, strip(r)],
+            near_send_sems.at[which, r],
+            near_recv_sems.at[which, r],
             mate,
         )
 
-    def far_copy(n):
+    def far_copy(r):
         return send(
-            far_send.at[:, column(n)],
-            far_recv.at[:, column(n)],
-            far_send_sems.at[n],
-            far_recv_sems.at[n],
+            far_send.at[strip(r)],
+            far_recv.at[strip(r)],
+            far_send_sems.at[r],
+            far_recv_sems.at[r],
             far,
         )
+
+    strips = tok // PIECE
 
     def mix(which, index):
         for n in range(width // SPAN):
@@ -407,21 +412,31 @@
             near_send[which, :, column(n)] = partial[block(1 - core), column(n)].astype(
                 jnp.bfloat16
             )
-            near_copy(which, n).start()
-
-    def reduced(which, n):
-        near_copy(which, n).wait_recv()
-        return partial[block(core), column(n)] + near_recv[which, :, column(n)].astype(
-            jnp.float32
+        for r in range(strips):
+            near_copy(which, r).start()
+
+    def reduced(which, r):
+        near_copy(which, r).wait_recv()
+        own = partial[pl.ds(pl.multiple_of(core * tok + r * PIECE, PIECE), PIECE), :]
+        return own + near_recv[which, strip(r), :].astype(jnp.float32)
+
+    def ring_piece(g, i):
+        rows = pl.ds(pl.multiple_of(OWN * tokens + i * PIECE, PIECE), PIECE)
+        to_rows = pl.ds(pl.multiple_of(g * tokens + i * PIECE, PIECE), PIECE)
+        return pltpu.make_async_remote_copy(
+            src_ref=blocks.at[rows],
+            dst_ref=blocks.at[to_rows],
+            send_sem=ring_send.at[g],
+            recv_sem=ring_recv.at[g],
+            device_id=(seq, along_ring(blk, core, SHIFTS[g])),
+            device_id_type=MESH,
         )
 
     attend(1 - half)
     mix(0, 1 - half)
-    for n in range(width // SPAN):
-        far_send[:, column(n)] = reduced(0, n).astype(jnp.bfloat16)
-        far_copy(n).start()
-    attend(half)
-    mix(1, half)
+    for r in range(strips):
+        far_send[strip(r), :] = reduced(0, r).astype(jnp.bfloat16)
+        far_copy(r).start()
     page = length // NPOS
     spread_owner = lax.div(
         lax.broadcasted_iota(jnp.int32, (NPOS, length), 1), page
@@ -449,30 +464,23 @@
     own_page.start()
     lax.fori_loop(1, NPOS, lambda j, _: (page_copy(j).start(), 0)[1], 0)
 
-    for n in range(width // SPAN):
-        mixed = reduced(1, n)
-        far_copy(n).wait_recv()
-        mixed = mixed + far_recv[:, column(n)].astype(jnp.float32)
-        resid[:, column(n)] = (rows_ref[:, column(n)].astype(jnp.float32) + mixed).astype(
-            jnp.bfloat16
-        )
-    blocks[own_rows, :] = norm(resid[...].astype(jnp.float32), ffn_gain_ref)
+    attend(half)
+    mix(1, half)
+    for r in range(strips):
+        mixed = reduced(1, r)
+        far_copy(r).wait_recv()
+        mixed = mixed + far_recv[strip(r), :].astype(jnp.float32)
+        summed = (rows_ref[strip(r), :].astype(jnp.float32) + mixed).astype(jnp.bfloat16)
+        resid[strip(r), :] = summed
+        blocks[pl.ds(OWN * tokens + r * PIECE, PIECE), :] = norm(
+            summed.astype(jnp.float32), ffn_gain_ref
+        )
+        for g in range(OWN):
+            ring_piece(g, r).start()
     own_out.wait_send()
     for i in range(PARTS):
         gather_out[i].wait_send()
         pass_out[i].wait_send()
-
-    def ring_piece(g, i):
-        rows = pl.ds(pl.multiple_of(OWN * tokens + i * PIECE, PIECE), PIECE)
-        to_rows = pl.ds(pl.multiple_of(g * tokens + i * PIECE, PIECE), PIECE)
-        return pltpu.make_async_remote_copy(
-            src_ref=blocks.at[rows],
-            dst_ref=blocks.at[to_rows],
-            send_sem=ring_send.at[g],
-            recv_sem=ring_recv.at[g],
-            device_id=(seq, along_ring(blk, core, SHIFTS[g])),
-            device_id_type=MESH,
-        )
 
     def ring_all(g):
         return pltpu.make_async_remote_copy(
@@ -573,8 +581,6 @@
 
     copies = (PLANE - 1) * (CAP // SUB)
     pieces = tokens // PIECE
-    for g in range(OWN):
-        lax.fori_loop(0, pieces, lambda i, _: (ring_piece(g, i).start(), 0)[1], 0)
     for g in range(RING):
         if g != OWN:
             ring_all(g).wait_recv()
@@ -667,10 +673,10 @@
             ring_all(g).wait_send()
             sum_all(g).wait_send()
     own_page.wait()
-    for n in range(width // SPAN):
-        near_copy(0, n).wait_send()
-        near_copy(1, n).wait_send()
-        far_copy(n).wait_send()
+    for r in range(strips):
+        near_copy(0, r).wait_send()
+        near_copy(1, r).wait_send()
+        far_copy(r).wait_send()
 
 
 def on_device(
@@ -696,7 +702,7 @@
     hbm = pl.BlockSpec(memory_space=pl.ANY)
     dma = pltpu.SemaphoreType.DMA
     bf16 = jnp.bfloat16
-    spans = width // SPAN
+    strips = tokens // PIECE
     residual_out, kv_cache = pl.pallas_call(
         layer_kernel,
         out_shape=(
@@ -743,10 +749,10 @@
             dma((PARTS,)),
             dma((PARTS,)),
             dma((PARTS,)),
-            dma((2, spans)),
-            dma((2, spans)),
-            dma((spans,)),
-            dma((spans,)),
+            dma((2, strips)),
+            dma((2, strips)),
+            dma((strips,)),
+            dma((strips,)),
             pltpu.VMEM((2, LOAD) + w_qkv.shape[1:], bf16),
             dma((2,)),
             dma((RING,)),

time: 155 us -> 148 us (0.955)
  the two profiles are of different devices: /device:TPU:40 before, /device:TPU:0 now
where the time goes in v6:
time: 148 us; the launch traced here: 145 us
  Pallas kernels  140 us (95%)
  local copies, waits for them, and re-layouts  4.19 us (3%)
    pallas_call x1, Pallas kernels, on_device(): pl.pallas_call(layer_kernel, out_shape=(jax.ShapeDtypeStruct((tokens, wid...  140 us
    unnamed x2, local copies, waits for them, and re-layouts  4.19 us

profile of v6, /device:TPU:0, one launch (start us, length us, event | category | flops | bytes accessed | tf_op | source)
XLA Modules:
  0.0 145.2 jit_solution(5721408675654171990)
XLA Ops:
  0.6 140.4 %shard_map.122 = (bf16[128,2048]{1,0:T(8,128)(2,1)}, bf16[32,16,1024]{2,1,0:T(8,128)(2,1)}) custom-call(bf16[128,2048]{1,0:T(8,128)(2,1)} %bitcast.14, s32[1,512]{1,0:T(1,128)} %segment_ref.1, s32[1,32]{1,0:T(1,128)} %owner_ref.1, bf16[2048]{0:T(1024)(128)(2,1)} %attn_gain_ref.1, bf16[2048]{0:T(1024)(128)(2,1)} %ffn_gain_ref.1, bf16[32,2048]{1,0:T(8,128)(2,1)} %bitcast.16, ...), custom_call_target="tpu_custom_call" | custom-call | tf_op jit(solution)/shard_map/pallas_call | solution.py:706
  141.0 1.9 %copy.15 = bf16[1,128,2048]{2,1,0:T(8,128)(2,1)} copy(bf16[1,128,2048]{2,1,0:T(8,128)(2,1)} %bitcast.15) | data formatting | bytes 1048576
  142.9 2.3 %copy.16 = bf16[1,32,16,1024]{3,2,1,0:T(8,128)(2,1)} copy(bf16[1,32,16,1024]{3,2,1,0:T(8,128)(2,1)} %bitcast.13) | data formatting | bytes 2097152

commit v7 on v6

--- a/solution.py
+++ b/solution.py
@@ -432,11 +432,6 @@
             device_id_type=MESH,
         )
 
-    attend(1 - half)
-    mix(0, 1 - half)
-    for r in range(strips):
-        far_send[strip(r), :] = reduced(0, r).astype(jnp.bfloat16)
-        far_copy(r).start()
     page = length // NPOS
     spread_owner = lax.div(
         lax.broadcasted_iota(jnp.int32, (NPOS, length), 1), page
@@ -464,6 +459,11 @@
     own_page.start()
     lax.fori_loop(1, NPOS, lambda j, _: (page_copy(j).start(), 0)[1], 0)
 
+    attend(1 - half)
+    mix(0, 1 - half)
+    for r in range(strips):
+        far_send[strip(r), :] = reduced(0, r).astype(jnp.bfloat16)
+        far_copy(r).start()
     attend(half)
     mix(1, half)
     for r in range(strips):
@@ -581,7 +581,7 @@
 
     copies = (PLANE - 1) * (CAP // SUB)
     pieces = tokens // PIECE
-    for g in range(RING):
+    for g in (OWN, 0, 1, 2):
         if g != OWN:
             ring_all(g).wait_recv()
         pack(g)

time: 148 us -> 145 us (0.980)
    pallas_call x1, Pallas kernels: 140 us -> 139 us  [on_device(): pl.pallas_call(layer_kernel, out_shape=(jax.ShapeDtypeStruct((tokens, wid...]
where the time goes in v7:
time: 145 us; the launch traced here: 143 us
  Pallas kernels  139 us (96%)
  local copies, waits for them, and re-layouts  4.19 us (3%)
    pallas_call x1, Pallas kernels, on_device(): pl.pallas_call(layer_kernel, out_shape=(jax.ShapeDtypeStruct((tokens, wid...  139 us
    unnamed x2, local copies, waits for them, and re-layouts  4.19 us

profile of v7, /device:TPU:0, one launch (start us, length us, event | category | flops | bytes accessed | tf_op | source)
XLA Modules:
  0.0 143.5 jit_solution(18210470861618642987)
XLA Ops:
  0.6 138.6 %shard_map.122 = (bf16[128,2048]{1,0:T(8,128)(2,1)}, bf16[32,16,1024]{2,1,0:T(8,128)(2,1)}) custom-call(bf16[128,2048]{1,0:T(8,128)(2,1)} %bitcast.14, s32[1,512]{1,0:T(1,128)} %segment_ref.1, s32[1,32]{1,0:T(1,128)} %owner_ref.1, bf16[2048]{0:T(1024)(128)(2,1)} %attn_gain_ref.1, bf16[2048]{0:T(1024)(128)(2,1)} %ffn_gain_ref.1, bf16[32,2048]{1,0:T(8,128)(2,1)} %bitcast.16, ...), custom_call_target="tpu_custom_call" | custom-call | tf_op jit(solution)/shard_map/pallas_call | solution.py:706
  139.3 1.9 %copy.15 = bf16[1,128,2048]{2,1,0:T(8,128)(2,1)} copy(bf16[1,128,2048]{2,1,0:T(8,128)(2,1)} %bitcast.15) | data formatting | bytes 1048576
  141.2 2.3 %copy.16 = bf16[1,32,16,1024]{3,2,1,0:T(8,128)(2,1)} copy(bf16[1,32,16,1024]{3,2,1,0:T(8,128)(2,1)} %bitcast.13) | data formatting | bytes 2097152

commit v8 on v7

--- a/solution.py
+++ b/solution.py
@@ -679,6 +679,29 @@
         far_copy(r).wait_send()
 
 
+def hand_over_kernel(rows_ref, pages_ref, out_ref, kv_ref, rows, pages, in_sems, out_sems):
+    moves = []
+    for which, (src, stage, dst) in enumerate(
+        [(rows_ref, rows, out_ref), (pages_ref, pages, kv_ref)]
+    ):
+        for i in range(4):
+            size = src.shape[0] // 4
+            part = slice(i * size, (i + 1) * size)
+            moves.append(
+                (
+                    pltpu.make_async_copy(src.at[part], stage.at[part], in_sems.at[which, i]),
+                    pltpu.make_async_copy(stage.at[part], dst.at[part], out_sems.at[which, i]),
+                )
+            )
+    for fetch, _ in moves:
+        fetch.start()
+    for fetch, put in moves:
+        fetch.wait()
+        put.start()
+    for _, put in moves:
+        put.wait()
+
+
 def on_device(
     residual_in,
     segment_ids,
@@ -778,6 +801,21 @@
         w_gate_up[0],
         w_down[0],
     )
+    residual_out, kv_cache = pl.pallas_call(
+        hand_over_kernel,
+        out_shape=(
+            jax.ShapeDtypeStruct(residual_out.shape, bf16),
+            jax.ShapeDtypeStruct(kv_cache.shape, bf16),
+        ),
+        in_specs=[hbm] * 2,
+        out_specs=(hbm, hbm),
+        scratch_shapes=[
+            pltpu.VMEM(residual_out.shape, bf16),
+            pltpu.VMEM(kv_cache.shape, bf16),
+            dma((2, 4)),
+            dma((2, 4)),
+        ],
+    )(residual_out, kv_cache)
     return (residual_out[None], kv_cache[None])
 
 

time: 145 us -> 143 us (0.986)
  local copies, waits for them, and re-layouts: 4.19 us -> 0 us
  Pallas kernels: 139 us -> 141 us
    unnamed x2 -> x0, local copies, waits for them, and re-layouts: 4.19 us -> none
    pallas_call x0 -> x1, Pallas kernels: none -> 2.31 us  [on_device(): pl.pallas_call(hand_over_kernel, out_shape=(jax.ShapeDtypeStruct(residual...]
where the time goes in v8:
time: 143 us; the launch traced here: 142 us
  Pallas kernels  141 us (99%)
    pallas_call x1, Pallas kernels, on_device(): pl.pallas_call(layer_kernel, out_shape=(jax.ShapeDtypeStruct((tokens, wid...  139 us

profile of v8, /device:TPU:0, one launch (start us, length us, event | category | flops | bytes accessed | tf_op | source)
XLA Modules:
  0.0 141.6 jit_solution(7016033855997131376)
XLA Ops:
  0.6 138.6 %shard_map.122 = (bf16[128,2048]{1,0:T(8,128)(2,1)}, bf16[32,16,1024]{2,1,0:T(8,128)(2,1)}) custom-call(bf16[128,2048]{1,0:T(8,128)(2,1)} %bitcast.13, s32[1,512]{1,0:T(1,128)} %segment_ref.1, s32[1,32]{1,0:T(1,128)} %owner_ref.1, bf16[2048]{0:T(1024)(128)(2,1)} %attn_gain_ref.1, bf16[2048]{0:T(1024)(128)(2,1)} %ffn_gain_ref.1, bf16[32,2048]{1,0:T(8,128)(2,1)} %bitcast.14, ...), custom_call_target="tpu_custom_call" | custom-call | tf_op jit(solution)/shard_map/pallas_call | solution.py:729
  139.3 2.3 %shard_map.123 = (bf16[128,2048]{1,0:T(8,128)(2,1)}, bf16[32,16,1024]{2,1,0:T(8,128)(2,1)}) custom-call(bf16[128,2048]{1,0:T(8,128)(2,1)} %get-tuple-element.6.rows_ref, bf16[32,16,1024]{2,1,0:T(8,128)(2,1)} %get-tuple-element.7.pages_ref), custom_call_target="tpu_custom_call" | custom-call | tf_op jit(solution)/shard_map/pallas_call | solution.py:804

commit v9 on v8

--- a/solution.py
+++ b/solution.py
@@ -22,7 +22,7 @@
 PARTS = 4
 SPAN = 512
 MESH = pl.DeviceIdType.MESH
-SHIFTS = (1, 3, 2, 0)
+SHIFTS = (2, 1, 3, 0)
 OWN = RING - 1
 
 
@@ -316,8 +316,6 @@
             load_qkv(i + 2).start()
 
     load_out.wait()
-    load_gate_up.start()
-    load_down.start()
     own_in.wait_recv()
     for i in range(PARTS // 2):
         gather_in[i].wait_recv()
@@ -464,6 +462,8 @@
     for r in range(strips):
         far_send[strip(r), :] = reduced(0, r).astype(jnp.bfloat16)
         far_copy(r).start()
+    load_gate_up.start()
+    load_down.start()
     attend(half)
     mix(1, half)
     for r in range(strips):

time: 143 us -> 143 us (level)
  no operation moved by 1% of the time
where the time goes in v9:
time: 143 us; the launch traced here: 140 us
  Pallas kernels  140 us (98%)
    pallas_call x1, Pallas kernels, on_device(): pl.pallas_call(layer_kernel, out_shape=(jax.ShapeDtypeStruct((tokens, wid...  137 us

profile of v9, /device:TPU:0, one launch (start us, length us, event | category | flops | bytes accessed | tf_op | source)
XLA Modules:
  0.0 140.3 jit_solution(1578688156909087473)
XLA Ops:
  0.6 137.4 %shard_map.122 = (bf16[128,2048]{1,0:T(8,128)(2,1)}, bf16[32,16,1024]{2,1,0:T(8,128)(2,1)}) custom-call(bf16[128,2048]{1,0:T(8,128)(2,1)} %bitcast.13, s32[1,512]{1,0:T(1,128)} %segment_ref.1, s32[1,32]{1,0:T(1,128)} %owner_ref.1, bf16[2048]{0:T(1024)(128)(2,1)} %attn_gain_ref.1, bf16[2048]{0:T(1024)(128)(2,1)} %ffn_gain_ref.1, bf16[32,2048]{1,0:T(8,128)(2,1)} %bitcast.14, ...), custom_call_target="tpu_custom_call" | custom-call | tf_op jit(solution)/shard_map/pallas_call | solution.py:729
  138.0 2.3 %shard_map.123 = (bf16[128,2048]{1,0:T(8,128)(2,1)}, bf16[32,16,1024]{2,1,0:T(8,128)(2,1)}) custom-call(bf16[128,2048]{1,0:T(8,128)(2,1)} %get-tuple-element.6.rows_ref, bf16[32,16,1024]{2,1,0:T(8,128)(2,1)} %get-tuple-element.7.pages_ref), custom_call_target="tpu_custom_call" | custom-call | tf_op jit(solution)/shard_map/pallas_call | solution.py:804
